TPU v7x, 256 devices: a whole 4x4x8 slice. The times are simulated.
256 devices in a mesh: ctx: 32 (over y, x, core), head: 8 (over z).
Axes of the slice: x: 4, y: 4, z: 8, core: 2. Of those that a mesh axis runs over, the one named last changes fastest.
Arguments:
- queries: bfloat16 [32768, 2048], P(('ctx', 'head')), may hold values from -6 to 6
- keys: bfloat16 [32768, 2048], P(('ctx', 'head')), may hold values from -6 to 6
- values: bfloat16 [32768, 2048], P(('ctx', 'head')), may hold values from -6 to 6
- grad_out: bfloat16 [32768, 2048], P(('ctx', 'head')), may hold values from -6 to 6
- gain: float32 [2048], replicated, may hold values from 0.1 to 1.9
- lengths: int32 [4], replicated, may hold values from 1 to 16384, 32768 in all
- block_mask: int32 [64, 6], P('ctx'), may hold values 0 or 1
Outputs:
- output: bfloat16 [32768, 2048], P(('ctx', 'head'))
- grad_queries: bfloat16 [32768, 2048], P(('ctx', 'head'))
- grad_keys: bfloat16 [32768, 2048], P(('ctx', 'head'))
- grad_values: bfloat16 [32768, 2048], P(('ctx', 'head'))
Inputs may be any that keep to these rules, and one draw needn't show every extreme that they name: The lengths of the 4 packed repertoires in order; they sum to 32768.
All inputs are finite; a program needn't handle non-finite values. No bound on the sum of `block_mask` on one device may be relied on, other than what follows from the above.
Results may differ from a plain program's by a relative error of at most 0.0051.
Values may be sent and summed in bfloat16 or wider, within the bound.
A program may use at most 64 MiB of HBM per device.

v0:
```python
import jax
import jax.numpy as jnp
from jax import lax
from jax.sharding import Mesh
from jax.sharding import PartitionSpec as P

HEADS = 16
DH = 128
GROUP = 512
CTX = ("ctx_0", "ctx_1", "ctx_2")
CTX_HEAD = ("ctx_0", "ctx_1", "ctx_2", "head")


eps_norm = 1e-06
pair_slots = [-1, -1, -1, -1, 0, -1, -1, -1, 1, 2, -1, -1, 3, 4, 5, -1]


def nothing_yet(value, identity):
    return jax.tree.map(
        lambda a, e: jnp.broadcast_to(jnp.asarray(e, a.dtype), a.shape), value, identity
    )


def carried_in(value, axes, combine, identity, reverse):
    before = start = nothing_yet(value, identity)
    subtotal = value
    for axis in reversed(axes):
        peers, mine = (lax.axis_size(axis), lax.axis_index(axis))
        pieces = jax.tree.map(lambda part: lax.all_gather(part, axis), subtotal)
        inside, subtotal = (start, start)
        for k in reversed(range(peers)) if reverse else range(peers):
            passed = k > mine if reverse else k < mine
            subtotal = combine(subtotal, jax.tree.map(lambda part: part[k], pieces))
            inside = jax.tree.map(lambda new, old: jnp.where(passed, new, old), subtotal, inside)
        before = combine(inside, before)
    return before


def segment_of(position, bounds):
    return jnp.sum((position[..., None] >= bounds).astype(jnp.int32), axis=-1)


def group_weights(mask_row, seg_group):
    full_side = seg_group.shape[0]
    quarter = full_side // 4
    select = (
        lax.broadcasted_iota(jnp.int32, (6, 16), 0)
        == jnp.array(pair_slots, dtype=jnp.int32)[None, :]
    ).astype(jnp.float32)
    blocks = jnp.dot(mask_row.astype(jnp.float32), select).reshape(4, 4) + jnp.eye(
        4, dtype=jnp.float32
    )
    spread = jnp.broadcast_to(blocks[:, None, :, None], (4, quarter, 4, quarter)).reshape(
        full_side, full_side
    )
    row_ids = lax.broadcasted_iota(jnp.int32, (full_side, full_side), 0)
    col_ids = lax.broadcasted_iota(jnp.int32, (full_side, full_side), 1)
    causal = (col_ids <= row_ids).astype(jnp.float32)
    shared = (seg_group[:, None] == seg_group[None, :]).astype(jnp.float32)
    return spread * causal * shared


def link_pair(first_part, second_part):
    return (first_part[0] * second_part[0], second_part[0] * first_part[1] + second_part[1])


def state_before(carry_prod, kv_local):
    identity = (jnp.ones((), jnp.float32), jnp.zeros_like(kv_local))
    prefix = carried_in((carry_prod, kv_local), CTX, link_pair, identity, False)
    result_state = prefix[1]
    return result_state


def state_after(carry_prod, grad_local):
    identity = (jnp.ones((), jnp.float32), jnp.zeros_like(grad_local))
    suffix = carried_in((carry_prod, grad_local), CTX, link_pair, identity, True)
    return suffix[1]


def local_link(carried, inputs):
    flag_now, update_now = inputs
    return ((carried[0] * flag_now, flag_now * carried[1] + update_now), carried)


def local(queries, keys, values, grad_out, gain, lengths, block_mask):
    q_head, k_head, v_head = (
        lax.all_to_all(queries, "head", split_axis=1, concat_axis=0, tiled=True),
        lax.all_to_all(keys, "head", split_axis=1, concat_axis=0, tiled=True),
        lax.all_to_all(values, "head", split_axis=1, concat_axis=0, tiled=True),
    )
    tok_rows = q_head.shape[0]
    local_cols = q_head.shape[1]
    local_heads = local_cols // DH
    group_count = tok_rows // GROUP
    full_width = HEADS * DH
    highest = lax.Precision.HIGHEST

    def blocked(source):
        return source.reshape(group_count, GROUP, local_heads, DH)

    bounds = jnp.cumsum(lengths)[:3]
    positions = lax.axis_index(CTX) * tok_rows + lax.iota(jnp.int32, tok_rows).reshape(
        group_count, GROUP
    )
    seg_ids = segment_of(positions, bounds)
    seg_before = segment_of(positions[:, 0] - 1, bounds)
    seg_after = segment_of(positions[:, -1] + 1, bounds)
    seg_start = seg_ids[:, 0]
    seg_end = seg_ids[:, -1]
    q_blocks = blocked(q_head)
    k_blocks = blocked(k_head)
    v_blocks = blocked(v_head)
    end_mask = (seg_ids == seg_end[:, None]).astype(jnp.bfloat16)
    updates = jnp.einsum(
        "cthi,cthj->chij",
        k_blocks * end_mask[:, :, None, None],
        v_blocks,
        preferred_element_type=jnp.float32,
    )
    carry_flags = (seg_end == seg_before).astype(jnp.float32)
    zero_state = jnp.zeros((local_heads, DH, DH), jnp.float32)
    device_sum, (flags_before, local_before) = lax.scan(
        local_link, (jnp.ones((), jnp.float32), zero_state), (carry_flags, updates)
    )
    kv_device = state_before(device_sum[0], device_sum[1])
    kv_states = flags_before[:, None, None, None] * kv_device[None] + local_before

    def forward_block(inputs):
        q_part, k_part, v_part, mask_row, seg_group, before_seg, kv_state = inputs
        weights = group_weights(mask_row, seg_group)
        before_mask = (seg_group == before_seg).astype(jnp.float32)
        scores = (
            jnp.einsum("thd,shd->hts", q_part, k_part, preferred_element_type=jnp.float32)
            * weights[None]
        )
        prob_bf = scores.astype(jnp.bfloat16)
        intra_term = jnp.einsum("hts,shd->thd", prob_bf, v_part, preferred_element_type=jnp.float32)
        inter_term = jnp.einsum(
            "thi,hij->thj", q_part.astype(jnp.float32), kv_state, precision=highest
        )
        return (intra_term + inter_term * before_mask[:, None, None]).astype(jnp.bfloat16)

    raw_head = lax.map(
        forward_block, (q_blocks, k_blocks, v_blocks, block_mask, seg_ids, seg_before, kv_states)
    ).reshape(tok_rows, local_cols)
    raw_tok = lax.all_to_all(raw_head, "head", split_axis=0, concat_axis=1, tiled=True)
    raw_float = raw_tok.astype(jnp.float32)
    scale_rms = jnp.sqrt(jnp.sum(raw_float * raw_float, axis=1) / full_width + eps_norm)
    normed = raw_float / scale_rms[:, None]
    output = (normed * gain[None, :]).astype(jnp.bfloat16)
    grad_norm = grad_out.astype(jnp.float32) * gain[None, :]
    cross_mean = jnp.sum(grad_norm * normed, axis=1) / full_width
    grad_raw = ((grad_norm - normed * cross_mean[:, None]) / scale_rms[:, None]).astype(
        jnp.bfloat16
    )
    d_flat = lax.all_to_all(grad_raw, "head", split_axis=1, concat_axis=0, tiled=True)
    d_blocks = blocked(d_flat)
    start_mask = (seg_ids == seg_start[:, None]).astype(jnp.bfloat16)
    grad_updates = jnp.einsum(
        "cthi,cthj->chij",
        q_blocks * start_mask[:, :, None, None],
        d_blocks,
        preferred_element_type=jnp.float32,
    )
    back_flags = (seg_start == seg_after).astype(jnp.float32)
    device_back, (flags_after, local_after) = lax.scan(
        local_link,
        (jnp.ones((), jnp.float32), zero_state),
        (back_flags, grad_updates),
        reverse=True,
    )
    grad_device = state_after(device_back[0], device_back[1])
    grad_states = flags_after[:, None, None, None] * grad_device[None] + local_after

    def backward_block(inputs):
        (
            q_part,
            k_part,
            v_part,
            d_part,
            mask_row,
            seg_group,
            before_seg,
            after_seg,
            kv_state,
            grad_state,
        ) = inputs
        weights = group_weights(mask_row, seg_group)
        before_mask = (seg_group == before_seg).astype(jnp.float32)
        after_mask = (seg_group == after_seg).astype(jnp.float32)
        prob_bf = (
            jnp.einsum("thd,shd->hts", q_part, k_part, preferred_element_type=jnp.float32)
            * weights[None]
        ).astype(jnp.bfloat16)
        grad_probs = (
            jnp.einsum("thd,shd->hts", d_part, v_part, preferred_element_type=jnp.float32)
            * weights[None]
        ).astype(jnp.bfloat16)
        grad_q = (
            jnp.einsum("hts,shd->thd", grad_probs, k_part, preferred_element_type=jnp.float32)
            + jnp.einsum("thj,hij->thi", d_part.astype(jnp.float32), kv_state, precision=highest)
            * before_mask[:, None, None]
        )
        grad_k = (
            jnp.einsum("hts,thd->shd", grad_probs, q_part, preferred_element_type=jnp.float32)
            + jnp.einsum("shj,hij->shi", v_part.astype(jnp.float32), grad_state, precision=highest)
            * after_mask[:, None, None]
        )
        grad_v = (
            jnp.einsum("hts,thd->shd", prob_bf, d_part, preferred_element_type=jnp.float32)
            + jnp.einsum("shi,hij->shj", k_part.astype(jnp.float32), grad_state, precision=highest)
            * after_mask[:, None, None]
        )
        return (
            grad_q.astype(jnp.bfloat16),
            grad_k.astype(jnp.bfloat16),
            grad_v.astype(jnp.bfloat16),
        )

    grad_blocks = lax.map(
        backward_block,
        (
            q_blocks,
            k_blocks,
            v_blocks,
            d_blocks,
            block_mask,
            seg_ids,
            seg_before,
            seg_after,
            kv_states,
            grad_states,
        ),
    )
    grad_q_head = grad_blocks[0].reshape(tok_rows, local_cols)
    grad_k_head = grad_blocks[1].reshape(tok_rows, local_cols)
    grad_v_head = grad_blocks[2].reshape(tok_rows, local_cols)
    back_q, back_k, back_v = (
        lax.all_to_all(grad_q_head, "head", split_axis=0, concat_axis=1, tiled=True),
        lax.all_to_all(grad_k_head, "head", split_axis=0, concat_axis=1, tiled=True),
        lax.all_to_all(grad_v_head, "head", split_axis=0, concat_axis=1, tiled=True),
    )
    return (output, back_q, back_k, back_v)


def solution(mesh):
    torus = Mesh(
        mesh.devices.reshape(4, 4, 2, mesh.shape["head"]), ("ctx_0", "ctx_1", "ctx_2", "head")
    )
    in_specs = (
        P(CTX_HEAD, None),
        P(CTX_HEAD, None),
        P(CTX_HEAD, None),
        P(CTX_HEAD, None),
        P(),
        P(),
        P(CTX, None),
    )
    out_specs = (P(CTX_HEAD, None), P(CTX_HEAD, None), P(CTX_HEAD, None), P(CTX_HEAD, None))
    return jax.shard_map(local, mesh=torus, in_specs=in_specs, out_specs=out_specs, check_vma=False)
```

profile of v0, /device:TPU:2, one launch (start us, length us, event | category | flops | bytes accessed | tf_op | source)
XLA Modules:
  0.0 347.6 jit_solution(1823683169859326135)
XLA Ops:
  0.6 1.9 copy.195
  2.5 8.6 %all-to-all-start.2 = ((bf16[128,8,256]{2,0,1:T(8,128)(2,1)}), bf16[128,8,256]{2,0,1:T(8,128)(2,1)S(1)}, u32[]{:S(2)}, u32[]{:S(2)}) async-start(bf16[128,8,256]{2,0,1:T(8,128)(2,1)} %bitcast.205), calls=%async_computation.2 | async-start | bytes 1048576 | tf_op jit(solution)/shard_map/all_to_all | solution.py:88
  12.3 16.3 %all-to-all-done.2 = bf16[128,8,256]{2,0,1:T(8,128)(2,1)S(1)} async-done(((bf16[128,8,256]{2,0,1:T(8,128)(2,1)}), bf16[128,8,256]{2,0,1:T(8,128)(2,1)S(1)}, u32[]{:S(2)}, u32[]{:S(2)}) %all-to-all-start.2) | async-done | bytes 524320 | tf_op jit(solution)/shard_map/all_to_all | solution.py:88
  28.6 3.6 %all-to-all-start = ((bf16[128,8,256]{2,0,1:T(8,128)(2,1)}), bf16[128,8,256]{2,0,1:T(8,128)(2,1)S(1)}, u32[]{:S(2)}, u32[]{:S(2)}) async-start(bf16[128,8,256]{2,0,1:T(8,128)(2,1)} %bitcast.207), calls=%async_computation | async-start | bytes 1048576 | tf_op jit(solution)/shard_map/all_to_all | solution.py:89
  35.2 14.9 %all-to-all-done = bf16[128,8,256]{2,0,1:T(8,128)(2,1)S(1)} async-done(((bf16[128,8,256]{2,0,1:T(8,128)(2,1)}), bf16[128,8,256]{2,0,1:T(8,128)(2,1)S(1)}, u32[]{:S(2)}, u32[]{:S(2)}) %all-to-all-start) | async-done | bytes 524320 | tf_op jit(solution)/shard_map/all_to_all | solution.py:89
  50.1 3.5 %all-to-all-start.1 = ((bf16[128,8,256]{2,0,1:T(8,128)(2,1)}), bf16[128,8,256]{2,0,1:T(8,128)(2,1)S(1)}, u32[]{:S(2)}, u32[]{:S(2)}) async-start(bf16[128,8,256]{2,0,1:T(8,128)(2,1)} %bitcast.206), calls=%async_computation.1 | async-start | bytes 1048576 | tf_op jit(solution)/shard_map/all_to_all | solution.py:87
  54.5 3.2 broadcast_multiply_fusion.1
  57.7 1.4 fusion.59
  59.2 4.1 %while.66 = (s32[]{:T(128)}, f32[]{:T(128)}, f32[2,128,128]{2,1,0:T(8,128)S(1)}, f32[2]{0:T(128)S(1)}, f32[2,2,128,128]{3,2,1,0:T(8,128)S(1)}, /*index=5*/f32[2]...) while((s32[]{:T(128)}, f32[]{:T(128)}, f32[2,128,128]{2,1,0:T(8,128)S(1)}, ...), condition=%wide.region_4.5_spmd.clone, body=%wide.region_3.4_spmd.clone.sunk | while | flops 131076 | bytes 655520 | solution.py:122
  64.7 2.4 all-reduce
  70.4 8.6 %all-reduce.1 = f32[4]{0:T(128)S(1)} all-reduce(f32[4]{0:T(128)S(1)} %dynamic-update-slice.1), channel_id=1, replica_groups=mesh['ctx_0'=4,'ctx_1'=4,'ctx_2'=2,'head'=8] {'ctx_1'}, use_global_device_ids=true, to_apply=%add.1 | all-reduce | flops 4 | bytes 32
  84.1 10.7 %all-reduce.2 = f32[4]{0:T(128)S(1)} all-reduce(f32[4]{0:T(128)S(1)} %dynamic-update-slice.2), channel_id=1, replica_groups=mesh['ctx_0'=4,'ctx_1'=4,'ctx_2'=2,'head'=8] {'ctx_0'}, use_global_device_ids=true, to_apply=%add.2 | all-reduce | flops 4 | bytes 32
  96.8 2.0 all-gather
  99.5 12.3 %all_gather.72 = f32[4,2,128,128]{3,2,1,0:T(8,128)S(1)} all-gather(f32[1,2,128,128]{3,2,1,0:T(8,128)S(1)} %fusion.70), channel_id=1, replica_groups=mesh['ctx_0'=4,'ctx_1'=4,'ctx_2'=2,'head'=8] {'ctx_1'}, dimensions={0}, use_global_device_ids=true | all-gather | bytes 655360 | tf_op jit(solution)/shard_map/all_gather | solution.py:29
  111.8 1.9 slice_add_fusion.14
  113.7 12.8 %all_gather.73 = f32[4,2,128,128]{3,2,1,0:T(8,128)S(1)} all-gather(f32[1,2,128,128]{3,2,1,0:T(8,128)S(1)} %slice_add_fusion.14), channel_id=1, replica_groups=mesh['ctx_0'=4,'ctx_1'=4,'ctx_2'=2,'head'=8] {'ctx_0'}, dimensions={0}, use_global_device_ids=true | all-gather | bytes 655360 | tf_op jit(solution)/shard_map/all_gather | solution.py:29
  127.3 4.5 %fusion.69 = f32[2,128,128]{2,1,0:T(8,128)S(1)} fusion(f32[4,2,128,128]{3,2,1,0:T(8,128)S(1)} %all_gather.73, f32[4,128,128]{2,1,0:T(8,128)S(1)} %all-gather, f32[4,2,128,128]{3,2,1,0:T(8,128)S(1)} %all_gather.72, f32[]{:T(128)S(6)} %mul.411, f32[]{:T(128)S(6)} %select_n.184, f32[]{:T(128)S(6)} %mul.409, f32[]{:T(128)} %bitcast.14, f32[]{:T(128)} %bitcast.21, ...), kind=kLoop, calls=%fused_computation.132 | loop fusion | flops 1015808 | bytes 1441850 | tf_op jit(solution)/shard_map/mul | solution.py:126
  132.9 13.5 %while.64 = (s32[]{:T(128)}, bf16[2,512,2,128]{3,2,1,0:T(2,128)(2,1)}, bf16[2,512,2,128]{3,2,1,0:T(2,128)(2,1)}, bf16[2,512,2,128]{3,2,1,0:T(2,128)(2,1)S(1)}, b...) while((s32[]{:T(128)}, ...), condition=%wide.region_6.7_spmd.clone, body=%wide.region_5.6_spmd.sunk.clone.sunk | while | flops 472253760 | bytes 9846321 | solution.py:143
  134.2 1.3 constant_dynamic-slice_fusion.16
  140.9 1.3 constant_dynamic-slice_fusion.16
  146.4 2.2 all_to_all.109
  148.6 7.1 %all-to-all-start.3 = ((bf16[8,128,256]{2,1,0:T(8,128)(2,1)}), bf16[8,128,256]{2,1,0:T(8,128)(2,1)S(1)}, u32[]{:S(2)}, u32[]{:S(2)}) async-start(bf16[8,128,256]{2,1,0:T(8,128)(2,1)} %all_to_all.109), calls=%async_computation.3 | async-start | bytes 1048576 | tf_op jit(solution)/shard_map/all_to_all | solution.py:146
  156.0 13.2 %all-to-all-done.3 = bf16[8,128,256]{2,1,0:T(8,128)(2,1)S(1)} async-done(((bf16[8,128,256]{2,1,0:T(8,128)(2,1)}), bf16[8,128,256]{2,1,0:T(8,128)(2,1)S(1)}, u32[]{:S(2)}, u32[]{:S(2)}) %all-to-all-start.3) | async-done | bytes 524320 | tf_op jit(solution)/shard_map/all_to_all | solution.py:146
  170.3 1.6 copy.130
  174.7 3.5 %all-to-all-start.4 = ((bf16[128,8,256]{2,0,1:T(8,128)(2,1)}), bf16[128,8,256]{2,0,1:T(8,128)(2,1)S(1)}, u32[]{:S(2)}, u32[]{:S(2)}) async-start(bf16[128,8,256]{2,0,1:T(8,128)(2,1)} %copy.132), calls=%async_computation.4 | async-start | bytes 1048576 | tf_op jit(solution)/shard_map/all_to_all | solution.py:156
  178.2 1.9 broadcast_multiply_fusion
  180.2 11.2 %all-to-all-done.4 = bf16[128,8,256]{2,0,1:T(8,128)(2,1)S(1)} async-done(((bf16[128,8,256]{2,0,1:T(8,128)(2,1)}), bf16[128,8,256]{2,0,1:T(8,128)(2,1)S(1)}, u32[]{:S(2)}, u32[]{:S(2)}) %all-to-all-start.4) | async-done | bytes 524320 | tf_op jit(solution)/shard_map/all_to_all | solution.py:156
  191.9 4.2 %while.67 = (s32[]{:T(128)}, f32[]{:T(128)}, f32[2,128,128]{2,1,0:T(8,128)S(1)}, f32[2]{0:T(128)S(1)}, f32[2,2,128,128]{3,2,1,0:T(8,128)S(1)}, /*index=5*/f32[2]...) while((s32[]{:T(128)}, f32[]{:T(128)}, f32[2,128,128]{2,1,0:T(8,128)S(1)}, ...), condition=%wide.region_11.12_spmd.clone, body=%wide.region_10.11_spmd.clone.sunk | while | flops 131077 | bytes 655532 | solution.py:166
  196.9 1.9 copy.124
  198.8 2.4 all-reduce.3
  204.0 11.1 %all-reduce.4 = f32[4]{0:T(128)S(1)} all-reduce(f32[4]{0:T(128)S(1)} %dynamic-update-slice.4), channel_id=1, replica_groups=mesh['ctx_0'=4,'ctx_1'=4,'ctx_2'=2,'head'=8] {'ctx_1'}, use_global_device_ids=true, to_apply=%add.4 | all-reduce | flops 4 | bytes 32
  220.2 8.3 %all-reduce.5 = f32[4]{0:T(128)S(1)} all-reduce(f32[4]{0:T(128)S(1)} %dynamic-update-slice.5), channel_id=1, replica_groups=mesh['ctx_0'=4,'ctx_1'=4,'ctx_2'=2,'head'=8] {'ctx_0'}, use_global_device_ids=true, to_apply=%add.5 | all-reduce | flops 4 | bytes 32
  230.5 2.0 all-gather.1
  233.8 12.1 %all_gather.82 = f32[4,2,128,128]{3,2,1,0:T(8,128)S(1)} all-gather(f32[1,2,128,128]{3,2,1,0:T(8,128)S(1)} %fusion.65), channel_id=1, replica_groups=mesh['ctx_0'=4,'ctx_1'=4,'ctx_2'=2,'head'=8] {'ctx_1'}, dimensions={0}, use_global_device_ids=true | all-gather | bytes 655360 | tf_op jit(solution)/shard_map/all_gather | solution.py:29
  245.9 1.8 slice_add_fusion.4
  247.7 12.8 %all_gather.83 = f32[4,2,128,128]{3,2,1,0:T(8,128)S(1)} all-gather(f32[1,2,128,128]{3,2,1,0:T(8,128)S(1)} %slice_add_fusion.4), channel_id=1, replica_groups=mesh['ctx_0'=4,'ctx_1'=4,'ctx_2'=2,'head'=8] {'ctx_0'}, dimensions={0}, use_global_device_ids=true | all-gather | bytes 655360 | tf_op jit(solution)/shard_map/all_gather | solution.py:29
  260.5 4.4 %fusion.64 = f32[2,128,128]{2,1,0:T(8,128)S(1)} fusion(f32[4,2,128,128]{3,2,1,0:T(8,128)S(1)} %all_gather.83, f32[4,128,128]{2,1,0:T(8,128)S(1)} %all-gather.1, f32[4,2,128,128]{3,2,1,0:T(8,128)S(1)} %all_gather.82, f32[]{:T(128)S(6)} %mul.451, f32[]{:T(128)S(6)} %select_n.210, f32[]{:T(128)S(6)} %mul.449, f32[]{:T(128)} %bitcast.36, f32[]{:T(128)} %bitcast.42, ...), kind=kLoop, calls=%fused_computation.117 | loop fusion | flops 1015808 | bytes 1441850 | tf_op jit(solution)/shard_map/mul | solution.py:173
  268.3 26.4 %while.65 = (s32[]{:T(128)}, bf16[2,512,2,128]{3,2,1,0:T(2,128)(2,1)}, bf16[2,512,2,128]{3,2,1,0:T(2,128)(2,1)}, bf16[2,512,2,128]{3,2,1,0:T(2,128)(2,1)}, bf16[...) while((s32[]{:T(128)}, ...), condition=%wide.region_13.14_spmd.clone, body=%wide.region_12.13_spmd.sunk.clone.sunk | while | flops 1279396096 | bytes 35284328 | solution.py:220
  269.7 1.3 compare_convert_fusion.13
  275.5 1.4 convolution_multiply_fusion.11
  288.7 1.4 convolution_multiply_fusion.11
  294.7 2.2 all_to_all.114
  296.9 3.5 %all-to-all-start.5 = ((bf16[8,128,256]{2,1,0:T(8,128)(2,1)}), bf16[8,128,256]{2,1,0:T(8,128)(2,1)S(1)}, u32[]{:S(2)}, u32[]{:S(2)}) async-start(bf16[8,128,256]{2,1,0:T(8,128)(2,1)} %all_to_all.114), calls=%async_computation.5 | async-start | bytes 1048576 | tf_op jit(solution)/shard_map/all_to_all | solution.py:239
  301.6 12.1 %all-to-all-done.5 = bf16[8,128,256]{2,1,0:T(8,128)(2,1)S(1)} async-done(((bf16[8,128,256]{2,1,0:T(8,128)(2,1)}), bf16[8,128,256]{2,1,0:T(8,128)(2,1)S(1)}, u32[]{:S(2)}, u32[]{:S(2)}) %all-to-all-start.5) | async-done | bytes 524320 | tf_op jit(solution)/shard_map/all_to_all | solution.py:239
  313.6 3.5 %all-to-all-start.6 = ((bf16[8,128,256]{2,1,0:T(8,128)(2,1)}), bf16[8,128,256]{2,1,0:T(8,128)(2,1)S(1)}, u32[]{:S(2)}, u32[]{:S(2)}) async-start(bf16[8,128,256]{2,1,0:T(8,128)(2,1)} %all_to_all.118), calls=%async_computation.6 | async-start | bytes 1048576 | tf_op jit(solution)/shard_map/all_to_all | solution.py:240
  318.3 11.4 %all-to-all-done.6 = bf16[8,128,256]{2,1,0:T(8,128)(2,1)S(1)} async-done(((bf16[8,128,256]{2,1,0:T(8,128)(2,1)}), bf16[8,128,256]{2,1,0:T(8,128)(2,1)S(1)}, u32[]{:S(2)}, u32[]{:S(2)}) %all-to-all-start.6) | async-done | bytes 524320 | tf_op jit(solution)/shard_map/all_to_all | solution.py:240
  329.6 3.5 %all-to-all-start.7 = ((bf16[8,128,256]{2,1,0:T(8,128)(2,1)}), bf16[8,128,256]{2,1,0:T(8,128)(2,1)S(1)}, u32[]{:S(2)}, u32[]{:S(2)}) async-start(bf16[8,128,256]{2,1,0:T(8,128)(2,1)} %all_to_all.122), calls=%async_computation.7 | async-start | bytes 1048576 | tf_op jit(solution)/shard_map/all_to_all | solution.py:241
  336.7 9.6 %all-to-all-done.7 = bf16[8,128,256]{2,1,0:T(8,128)(2,1)S(1)} async-done(((bf16[8,128,256]{2,1,0:T(8,128)(2,1)}), bf16[8,128,256]{2,1,0:T(8,128)(2,1)S(1)}, u32[]{:S(2)}, u32[]{:S(2)}) %all-to-all-start.7) | async-done | bytes 524320 | tf_op jit(solution)/shard_map/all_to_all | solution.py:241
  (224 shorter events, 70.7 us)
Async XLA Ops:
  2.5 8.8 %copy-start.12 = (bf16[128,2048]{1,0:T(8,128)(2,1)S(1)}, bf16[128,2048]{1,0:T(8,128)(2,1)}, u32[]{:S(2)}) copy-start(bf16[128,2048]{1,0:T(8,128)(2,1)} %param.19) | copy-start | bytes 1572868
  2.5 26.1 %all-to-all-start.2 = ((bf16[128,8,256]{2,0,1:T(8,128)(2,1)}), bf16[128,8,256]{2,0,1:T(8,128)(2,1)S(1)}, u32[]{:S(2)}, u32[]{:S(2)}) async-start(bf16[128,8,256]{2,0,1:T(8,128)(2,1)} %bitcast.205), calls=%async_computation.2 | async-start | bytes 1048576 | tf_op jit(solution)/shard_map/all_to_all | solution.py:88
  11.1 1.0 copy-start.18
  11.3 21.1 %copy-start.13 = (bf16[128,2048]{1,0:T(8,128)(2,1)S(1)}, bf16[128,2048]{1,0:T(8,128)(2,1)}, u32[]{:S(2)}) copy-start(bf16[128,2048]{1,0:T(8,128)(2,1)} %param.17) | copy-start | bytes 1572868
  28.6 4.6 %copy-start.21 = (u32[256]{0:T(256)S(1)}, u32[256]{0:T(256)}, u32[]{:S(2)}) copy-start(u32[256]{0:T(256)} %constant.144) | copy-start | bytes 3076
  28.6 21.5 %all-to-all-start = ((bf16[128,8,256]{2,0,1:T(8,128)(2,1)}), bf16[128,8,256]{2,0,1:T(8,128)(2,1)S(1)}, u32[]{:S(2)}, u32[]{:S(2)}) async-start(bf16[128,8,256]{2,0,1:T(8,128)(2,1)} %bitcast.207), calls=%async_computation | async-start | bytes 1048576 | tf_op jit(solution)/shard_map/all_to_all | solution.py:89
  50.1 76.4 %all-to-all-start.1 = ((bf16[128,8,256]{2,0,1:T(8,128)(2,1)}), bf16[128,8,256]{2,0,1:T(8,128)(2,1)S(1)}, u32[]{:S(2)}, u32[]{:S(2)}) async-start(bf16[128,8,256]{2,0,1:T(8,128)(2,1)} %bitcast.206), calls=%async_computation.1 | async-start | bytes 1048576 | tf_op jit(solution)/shard_map/all_to_all | solution.py:87
  59.1 4.9 %copy-start.20 = (u32[256]{0:T(256)S(1)}, u32[256]{0:T(256)}, u32[]{:S(2)}) copy-start(u32[256]{0:T(256)} %constant.149) | copy-start | bytes 3076
  59.1 10.7 %copy-start.19 = (u32[256]{0:T(256)S(1)}, u32[256]{0:T(256)}, u32[]{:S(2)}) copy-start(u32[256]{0:T(256)} %constant.154) | copy-start | bytes 3076
  127.2 5.7 %copy-start.15 = (s32[16]{0:T(128)S(1)}, s32[16]{0:T(128)}, u32[]{:S(2)}) copy-start(s32[16]{0:T(128)} %constant.136.clone..sunk.4) | copy-start | bytes 196
  127.3 5.7 %copy-start.17 = (s32[2,6]{1,0:T(2,128)S(1)}, s32[2,6]{1,0:T(2,128)}, u32[]{:S(2)}) copy-start(s32[2,6]{1,0:T(2,128)} %param.23) | copy-start | bytes 148
  146.4 9.4 %copy-start.14 = (bf16[128,2048]{1,0:T(8,128)(2,1)S(1)}, bf16[128,2048]{1,0:T(8,128)(2,1)}, u32[]{:S(2)}) copy-start(bf16[128,2048]{1,0:T(8,128)(2,1)} %param.20) | copy-start | bytes 1572868
  148.6 20.6 %all-to-all-start.3 = ((bf16[8,128,256]{2,1,0:T(8,128)(2,1)}), bf16[8,128,256]{2,1,0:T(8,128)(2,1)S(1)}, u32[]{:S(2)}, u32[]{:S(2)}) async-start(bf16[8,128,256]{2,1,0:T(8,128)(2,1)} %all_to_all.109), calls=%async_computation.3 | async-start | bytes 1048576 | tf_op jit(solution)/shard_map/all_to_all | solution.py:146
  170.3 1.8 copy-start.16
  174.7 16.7 %all-to-all-start.4 = ((bf16[128,8,256]{2,0,1:T(8,128)(2,1)}), bf16[128,8,256]{2,0,1:T(8,128)(2,1)S(1)}, u32[]{:S(2)}, u32[]{:S(2)}) async-start(bf16[128,8,256]{2,0,1:T(8,128)(2,1)} %copy.132), calls=%async_computation.4 | async-start | bytes 1048576 | tf_op jit(solution)/shard_map/all_to_all | solution.py:156
  268.3 4.9 %copy-start = (bf16[2,512,2,128]{3,2,1,0:T(2,128)(2,1)}, bf16[2,512,2,128]{3,2,1,0:T(2,128)(2,1)S(1)}, u32[]{:S(2)}) copy-start(bf16[2,512,2,128]{3,2,1,0:T(2,128)(2,1)S(1)} %get-tuple-element.1047) | copy-start | bytes 1572868 | tf_op jit(solution)/shard_map/while
  268.3 4.9 %copy-start.3 = (f32[2,2,128,128]{3,2,1,0:T(8,128)}, f32[2,2,128,128]{3,2,1,0:T(8,128)S(1)}, u32[]{:S(2)}) copy-start(f32[2,2,128,128]{3,2,1,0:T(8,128)S(1)} %get-tuple-element.1045) | copy-start | bytes 786436 | tf_op jit(solution)/shard_map/while
  268.3 7.2 %copy-start.5 = (f32[2,2,128,128]{3,2,1,0:T(8,128)}, f32[2,2,128,128]{3,2,1,0:T(8,128)S(1)}, u32[]{:S(2)}) copy-start(f32[2,2,128,128]{3,2,1,0:T(8,128)S(1)} %get-tuple-element.1048) | copy-start | bytes 786436 | tf_op jit(solution)/shard_map/while
  275.5 1.4 copy-start.2
  277.4 1.0 copy-start.8
  277.7 1.8 copy-start.4
  279.5 0.9 copy-start.9
  280.4 1.1 copy-start.1
  280.4 1.1 copy-start.6
  281.5 4.9 %copy-start = (bf16[2,512,2,128]{3,2,1,0:T(2,128)(2,1)}, bf16[2,512,2,128]{3,2,1,0:T(2,128)(2,1)S(1)}, u32[]{:S(2)}) copy-start(bf16[2,512,2,128]{3,2,1,0:T(2,128)(2,1)S(1)} %get-tuple-element.1047) | copy-start | bytes 1572868 | tf_op jit(solution)/shard_map/while
  281.5 4.9 %copy-start.3 = (f32[2,2,128,128]{3,2,1,0:T(8,128)}, f32[2,2,128,128]{3,2,1,0:T(8,128)S(1)}, u32[]{:S(2)}) copy-start(f32[2,2,128,128]{3,2,1,0:T(8,128)S(1)} %get-tuple-element.1045) | copy-start | bytes 786436 | tf_op jit(solution)/shard_map/while
  281.5 7.2 %copy-start.5 = (f32[2,2,128,128]{3,2,1,0:T(8,128)}, f32[2,2,128,128]{3,2,1,0:T(8,128)S(1)}, u32[]{:S(2)}) copy-start(f32[2,2,128,128]{3,2,1,0:T(8,128)S(1)} %get-tuple-element.1048) | copy-start | bytes 786436 | tf_op jit(solution)/shard_map/while
  288.7 1.4 copy-start.2
  290.6 1.0 copy-start.8
  290.9 1.8 copy-start.4
  292.7 0.9 copy-start.9
  293.6 1.1 copy-start.1
  293.6 1.1 copy-start.6
  294.7 5.7 %copy-start.10 = (bf16[2,512,2,128]{3,2,1,0:T(2,128)(2,1)S(1)}, bf16[2,512,2,128]{3,2,1,0:T(2,128)(2,1)}, u32[]{:S(2)}) copy-start(bf16[2,512,2,128]{3,2,1,0:T(2,128)(2,1)} %get-tuple-element.329) | copy-start | bytes 1572868
  296.9 16.7 %all-to-all-start.5 = ((bf16[8,128,256]{2,1,0:T(8,128)(2,1)}), bf16[8,128,256]{2,1,0:T(8,128)(2,1)S(1)}, u32[]{:S(2)}, u32[]{:S(2)}) async-start(bf16[8,128,256]{2,1,0:T(8,128)(2,1)} %all_to_all.114), calls=%async_computation.5 | async-start | bytes 1048576 | tf_op jit(solution)/shard_map/all_to_all | solution.py:239
  300.4 16.7 %copy-start.11 = (bf16[2,512,2,128]{3,2,1,0:T(2,128)(2,1)S(1)}, bf16[2,512,2,128]{3,2,1,0:T(2,128)(2,1)}, u32[]{:S(2)}) copy-start(bf16[2,512,2,128]{3,2,1,0:T(2,128)(2,1)} %get-tuple-element.330) | copy-start | bytes 1572868
  313.6 16.0 %all-to-all-start.6 = ((bf16[8,128,256]{2,1,0:T(8,128)(2,1)}), bf16[8,128,256]{2,1,0:T(8,128)(2,1)S(1)}, u32[]{:S(2)}, u32[]{:S(2)}) async-start(bf16[8,128,256]{2,1,0:T(8,128)(2,1)} %all_to_all.118), calls=%async_computation.6 | async-start | bytes 1048576 | tf_op jit(solution)/shard_map/all_to_all | solution.py:240
  317.1 16.0 %copy-start.7 = (bf16[128,2048]{0,1:T(8,128)(2,1)S(1)}, bf16[128,2048]{0,1:T(8,128)(2,1)}, u32[]{:S(2)}) copy-start(bf16[128,2048]{0,1:T(8,128)(2,1)} %get-tuple-element.652) | copy-start | bytes 1572868
  329.6 16.7 %all-to-all-start.7 = ((bf16[8,128,256]{2,1,0:T(8,128)(2,1)}), bf16[8,128,256]{2,1,0:T(8,128)(2,1)S(1)}, u32[]{:S(2)}, u32[]{:S(2)}) async-start(bf16[8,128,256]{2,1,0:T(8,128)(2,1)} %all_to_all.122), calls=%async_computation.7 | async-start | bytes 1048576 | tf_op jit(solution)/shard_map/all_to_all | solution.py:241
where the time goes:
time: 350 us; the launch traced here: 348 us
  blocking collectives  97.7 us (28%)
  waiting for transfers between devices  88.6 us (25%)
  local copies, waits for them, and re-layouts  63.3 us (18%)
  starting transfers between devices  36.8 us (11%)
  other arithmetic  30.3 us (9%)
  between operations  15 us (4%)
  matrix products  12.7 us (4%)
    all_gather x6, blocking collectives, carried_in(): pieces = jax.tree.map(lambda part: lax.all_gather(part, axis), subtotal)  53.9 us
    unnamed x6, blocking collectives  43.7 us
    all_to_all x1, waiting for transfers between devices, local(): lax.all_to_all(keys, 'head', split_axis=1, concat_axis=0, tiled=True)  16.3 us
    all_to_all x1, waiting for transfers between devices, local(): lax.all_to_all(values, 'head', split_axis=1, concat_axis=0, tiled=True)  14.9 us
    dynamic_slice x24, local copies, waits for them, and re-layouts, local(): lax.map(forward_block, (q_blocks, k_blocks, v_blocks, block_mask, seg_ids...  14.3 us
    all_to_all x1, waiting for transfers between devices, local(): lax.all_to_all(raw_head, 'head', split_axis=0, concat_axis=1, tiled=True)  13.2 us
    all_to_all x1, waiting for transfers between devices, local(): lax.all_to_all(grad_q_head, 'head', split_axis=0, concat_axis=1, tiled=True)  12.1 us
    all_to_all x1, waiting for transfers between devices, local(): lax.all_to_all(grad_k_head, 'head', split_axis=0, concat_axis=1, tiled=True)  11.4 us
  transfers between devices with their start and end apart: 8, of which 7 were waited for; matrix products, arithmetic and copies ran while one was open for 8% of the time, Pallas kernels for 0%

commit v1 on v0

v1 whole, which is shorter than its diff:
```python
import jax
import jax.numpy as jnp
from jax import lax
from jax.experimental import pallas as pl
from jax.experimental.pallas import tpu as pltpu
from jax.sharding import Mesh
from jax.sharding import PartitionSpec as P

HEADS = 16
DH = 128
GROUP = 512
BLOCK = 128
EPS = 1e-06
F32 = jnp.float32
BF16 = jnp.bfloat16
TOKEN_AXES = ("cy", "cx", "cc", "head")
NY, NX, NC, NZ = 4, 4, 2, 8
CHIP = NC * NZ
MESH_ID = pl.DeviceIdType.MESH
CHUNKS = 2
ROWS = DH // CHUNKS


def mm(a, b, dims):
    return lax.dot_general(a, b, (dims, ((), ())), preferred_element_type=F32)


NN = ((1,), (0,))
NT = ((1,), (1,))
TN = ((0,), (0,))


def kernel(
    lengths, block_mask, q_ref, k_ref, v_ref, go_ref, gain_ref,
    out_ref, gq_ref, gk_ref, gv_ref,
    mask_mine, mask_all, probs, gprobs, diag, acc_k, acc_v, d_ref,
    m_loc, m_own, x_own, x_loc, n_loc, n_own, y_own, y_loc,
    tot_x, rec_x, tot_y, rec_y,
    a_send, a_recv, b_send, b_recv, x_send, x_recv, y_send, y_recv, mask_send, mask_recv,
):
    iy, ix, ic, iz = (lax.axis_index(a) for a in TOKEN_AXES)
    chip = iy * NX + ix
    mine = ic * NZ + iz
    owner = iz * NC + ic
    base = chip * (CHIP * BLOCK)
    start = base + mine * BLOCK

    barrier = pltpu.get_barrier_semaphore()

    def peer(step):
        e = lax.rem(owner + step, CHIP)
        return e, {"head": e // NC, "cc": lax.rem(e, NC)}

    def greet(step, carry):
        pl.semaphore_signal(barrier, 1, device_id=peer(step)[1], device_id_type=MESH_ID)
        return carry

    lax.fori_loop(1, CHIP, greet, 0)
    for step in range(1, NX):
        pl.semaphore_signal(
            barrier, 1, device_id={"cx": lax.rem(ix + step, NX)}, device_id_type=MESH_ID
        )
    for step in range(1, NY):
        pl.semaphore_signal(
            barrier, 1, device_id={"cy": lax.rem(iy + step, NY)}, device_id_type=MESH_ID
        )

    b1 = lengths[0]
    b2 = b1 + lengths[1]
    b3 = b2 + lengths[2]

    def seg(p):
        return (
            (p >= b1).astype(jnp.int32) + (p >= b2).astype(jnp.int32) + (p >= b3).astype(jnp.int32)
        )

    def same(a, b):
        return (a == b).astype(F32)

    for g in range(2):
        for n in range(6):
            mask_mine[8 * g + n : 8 * g + n + 1, :] = jnp.full(
                (1, DH), block_mask[g, n].astype(F32), F32
            )

    rows = lax.broadcasted_iota(jnp.int32, (BLOCK, BLOCK), 0)
    cols = lax.broadcasted_iota(jnp.int32, (BLOCK, BLOCK), 1)
    seg_r = seg(start + rows)
    seg_c = seg(start + cols)
    weight = jnp.where((seg_r == seg_c) & (cols <= rows), 1.0, 0.0).astype(F32)
    ends = jnp.where(seg_r == seg(start + BLOCK - 1), 1.0, 0.0).astype(BF16)
    starts = jnp.where(seg_r == seg(start), 1.0, 0.0).astype(BF16)
    before = jnp.where(seg_r == seg(start - 1), 1.0, 0.0).astype(BF16)
    after = jnp.where(seg_r == seg(start + BLOCK), 1.0, 0.0).astype(BF16)

    def col(h):
        return slice(h * DH, (h + 1) * DH)

    for h in range(HEADS):
        m_loc[h] = mm(k_ref[:, col(h)] * ends, v_ref[:, col(h)], TN).astype(BF16)

    pl.semaphore_wait(barrier, CHIP - 1 + NX - 1 + NY - 1)

    mask_copy = pltpu.make_async_remote_copy(
        src_ref=mask_mine,
        dst_ref=mask_all.at[ic],
        send_sem=mask_send,
        recv_sem=mask_recv,
        device_id={"cc": 1 - ic},
        device_id_type=MESH_ID,
    )
    mask_copy.start()
    mask_all[ic] = mask_mine[...]

    def chunk(c):
        return pl.ds(c * ROWS, ROWS)

    def scatter_copy(src, dst, c, step, phase):
        e, to = peer(step)
        return pltpu.make_async_remote_copy(
            src_ref=src.at[e, chunk(c)],
            dst_ref=dst.at[mine, chunk(c)],
            send_sem=a_send.at[phase, c, e],
            recv_sem=a_recv.at[phase, c, mine],
            device_id=to,
            device_id_type=MESH_ID,
        )

    def gather_copy(src, dst, c, step, phase):
        e, to = peer(step)
        r = lax.rem(e, NC) * NZ + e // NC
        return pltpu.make_async_remote_copy(
            src_ref=src.at[r, chunk(c)],
            dst_ref=dst.at[owner, chunk(c)],
            send_sem=b_send.at[phase, c, e],
            recv_sem=b_recv.at[phase, c, owner],
            device_id=to,
            device_id_type=MESH_ID,
        )

    def start_scatter(src, dst, phase):
        for c in range(CHUNKS):

            def go(step, carry):
                scatter_copy(src, dst, c, step, phase).start()
                return carry

            lax.fori_loop(1, CHIP, go, 0)
        dst[mine] = src[owner]

    def wait_scatter(src, dst, c, phase):
        def take(step, carry):
            e, to = peer(step)
            r = lax.rem(e, NC) * NZ + e // NC
            pltpu.make_async_remote_copy(
                src_ref=src.at[e, chunk(c)],
                dst_ref=dst.at[r, chunk(c)],
                send_sem=a_send.at[phase, c, e],
                recv_sem=a_recv.at[phase, c, r],
                device_id=to,
                device_id_type=MESH_ID,
            ).wait()
            return carry

        lax.fori_loop(1, CHIP, take, 0)

    def start_gather(src, dst, c, phase):
        def go(step, carry):
            gather_copy(src, dst, c, step, phase).start()
            return carry

        lax.fori_loop(1, CHIP, go, 0)
        dst[owner, chunk(c)] = src[mine, chunk(c)]

    def wait_gather(src, dst, c, phase):
        def take(step, carry):
            e, to = peer(step)
            r = lax.rem(e, NC) * NZ + e // NC
            pltpu.make_async_remote_copy(
                src_ref=src.at[r, chunk(c)],
                dst_ref=dst.at[e, chunk(c)],
                send_sem=b_send.at[phase, c, e],
                recv_sem=b_recv.at[phase, c, e],
                device_id=to,
                device_id_type=MESH_ID,
            ).wait()
            return carry

        lax.fori_loop(1, CHIP, take, 0)

    def line_copy(total, slots, c, phase, axis, me, to, slot, send, recv):
        return pltpu.make_async_remote_copy(
            src_ref=total.at[phase, chunk(c)],
            dst_ref=slots.at[phase, slot, chunk(c)],
            send_sem=send.at[phase, c, to],
            recv_sem=recv.at[phase, c, slot],
            device_id={axis: to},
            device_id_type=MESH_ID,
        )

    def exchange(total, slots, c, phase, axis, me, size, send, recv):
        for step in range(1, size):
            to = lax.rem(me + step, size)
            line_copy(total, slots, c, phase, axis, me, to, me, send, recv).start()
        slots[phase, me, chunk(c)] = total[phase, chunk(c)]
        for step in range(1, size):
            to = lax.rem(me + step, size)
            line_copy(total, slots, c, phase, axis, me, to, to, send, recv).wait()

    def states(own, result, c, phase):
        forward = phase == 0
        lo = [base + r * BLOCK for r in range(CHIP)]
        edge = [seg(p + BLOCK - 1) if forward else seg(p) for p in lo]
        want = [seg(p - 1) if forward else seg(p + BLOCK) for p in lo]
        last = CHIP - 1 if forward else 0
        chip_len = CHIP * BLOCK
        row_len = NX * chip_len
        row_at = iy * row_len
        enter = seg(base - 1) if forward else seg(base + chip_len)

        def edge_of(at, size):
            return seg(at + size - 1) if forward else seg(at)

        def block(r):
            return own[r, chunk(c)].astype(F32)

        total = block(last)
        for r in range(CHIP):
            if r != last:
                total += same(edge[r], edge[last]) * block(r)
        tot_x[phase, chunk(c)] = total
        exchange(tot_x, rec_x, c, phase, "cx", ix, NX, x_send, x_recv)
        row_edge = edge_of(row_at, row_len)
        row_total = jnp.zeros((ROWS, DH), F32)
        state = jnp.zeros((ROWS, DH), F32)
        for x in range(NX):
            part = rec_x[phase, x, chunk(c)]
            its = edge_of(row_at + x * chip_len, chip_len)
            row_total += same(its, row_edge) * part
            passed = (x < ix) if forward else (x > ix)
            state += same(its, enter) * passed.astype(F32) * part
        tot_y[phase, chunk(c)] = row_total
        exchange(tot_y, rec_y, c, phase, "cy", iy, NY, y_send, y_recv)
        for y in range(NY):
            its = edge_of(y * row_len, row_len)
            passed = (y < iy) if forward else (y > iy)
            state += same(its, enter) * passed.astype(F32) * rec_y[phase, y, chunk(c)]
        groups = range(CHIP // 4)
        reach = enter
        for g in groups if forward else reversed(groups):
            inner = range(4) if forward else (3, 2, 1, 0)
            seen = []
            for i in inner:
                r = 4 * g + i
                value = same(reach, want[r]) * state
                for j in seen:
                    hi, lo_ = (i, j) if forward else (j, i)
                    slot = 8 * (g % 2) + hi * (hi - 1) // 2 + lo_
                    pair = mask_all[g // 2, slot : slot + 1, :] * same(edge[4 * g + j], want[r])
                    value += pair * block(4 * g + j)
                result[r, chunk(c)] = value.astype(BF16)
                seen.append(i)
            far = 4 * g + (3 if forward else 0)
            state = same(reach, edge[far]) * state
            for i in inner:
                state += same(edge[4 * g + i], edge[far]) * block(4 * g + i)
            reach = edge[far]

    start_scatter(m_loc, m_own, 0)
    for h in range(HEADS):
        p = (mm(q_ref[:, col(h)], k_ref[:, col(h)], NT) * weight).astype(BF16)
        probs[h] = p
        diag[:, col(h)] = mm(p, v_ref[:, col(h)], NN)
    mask_copy.wait()
    for c in range(CHUNKS):
        wait_scatter(m_loc, m_own, c, 0)
        states(m_own, x_own, c, 0)
        start_gather(x_own, x_loc, c, 0)
    for c in range(CHUNKS):
        wait_gather(x_own, x_loc, c, 0)

    total_sq = jnp.zeros((BLOCK, DH), F32)
    total_gr = jnp.zeros((BLOCK, DH), F32)
    for h in range(HEADS):
        raw = (
            diag[:, col(h)] + mm(q_ref[:, col(h)] * before, x_loc[h], NN)
        ).astype(BF16).astype(F32)
        diag[:, col(h)] = raw
        scaled = go_ref[:, col(h)].astype(F32) * gain_ref[:, col(h)]
        total_sq += raw * raw
        total_gr += scaled * raw
    width = HEADS * DH
    inv = 1.0 / jnp.sqrt(jnp.sum(total_sq, axis=1, keepdims=True) / width + EPS)
    cross = jnp.sum(total_gr, axis=1, keepdims=True) * inv / width
    for h in range(HEADS):
        normed = diag[:, col(h)] * inv
        scaled = go_ref[:, col(h)].astype(F32) * gain_ref[:, col(h)]
        out_ref[:, col(h)] = (normed * gain_ref[:, col(h)]).astype(BF16)
        d = ((scaled - normed * cross) * inv).astype(BF16)
        d_ref[:, col(h)] = d
        n_loc[h] = mm(q_ref[:, col(h)] * starts, d, TN).astype(BF16)
    start_scatter(n_loc, n_own, 1)

    for h in range(HEADS):
        d = d_ref[:, col(h)]
        gp = (mm(d, v_ref[:, col(h)], NT) * weight).astype(BF16)
        gq_ref[:, col(h)] = (
            mm(gp, k_ref[:, col(h)], NN) + mm(d * before, x_loc[h], NT)
        ).astype(BF16)
        acc_k[:, col(h)] = mm(gp, q_ref[:, col(h)], TN)
        acc_v[:, col(h)] = mm(probs[h], d, TN)
    for c in range(CHUNKS):
        wait_scatter(n_loc, n_own, c, 1)
        states(n_own, y_own, c, 1)
        start_gather(y_own, y_loc, c, 1)
    for c in range(CHUNKS):
        wait_gather(y_own, y_loc, c, 1)
    for h in range(HEADS):
        y = y_loc[h]
        gk_ref[:, col(h)] = (acc_k[:, col(h)] + mm(v_ref[:, col(h)] * after, y, NT)).astype(BF16)
        gv_ref[:, col(h)] = (acc_v[:, col(h)] + mm(k_ref[:, col(h)] * after, y, NN)).astype(BF16)


def local(queries, keys, values, grad_out, gain, lengths, block_mask):
    shape = queries.shape
    vmem = pl.BlockSpec(memory_space=pltpu.VMEM)
    smem = pl.BlockSpec(memory_space=pltpu.SMEM)
    square = (HEADS, DH, DH)
    dma = pltpu.SemaphoreType.DMA
    return pl.pallas_call(
        kernel,
        out_shape=[jax.ShapeDtypeStruct(shape, BF16)] * 4,
        in_specs=[smem, smem, vmem, vmem, vmem, vmem, vmem],
        out_specs=[vmem] * 4,
        scratch_shapes=[
            pltpu.VMEM((16, DH), F32),
            pltpu.VMEM((2, 16, DH), F32),
            pltpu.VMEM(square, BF16),
            pltpu.VMEM((8, DH), BF16),
            pltpu.VMEM(shape, F32),
            pltpu.VMEM(shape, F32),
            pltpu.VMEM(shape, F32),
            pltpu.VMEM(shape, BF16),
        ]
        + [pltpu.VMEM(square, BF16)] * 8
        + [
            pltpu.VMEM((2, DH, DH), F32),
            pltpu.VMEM((2, NX, DH, DH), F32),
            pltpu.VMEM((2, DH, DH), F32),
            pltpu.VMEM((2, NY, DH, DH), F32),
            dma((2, CHUNKS, CHIP)),
            dma((2, CHUNKS, CHIP)),
            dma((2, CHUNKS, CHIP)),
            dma((2, CHUNKS, CHIP)),
            dma((2, CHUNKS, NX)),
            dma((2, CHUNKS, NX)),
            dma((2, CHUNKS, NY)),
            dma((2, CHUNKS, NY)),
            dma,
            dma,
        ],
        compiler_params=pltpu.CompilerParams(
            collective_id=0, has_side_effects=True, vmem_limit_bytes=40 * 1024 * 1024
        ),
    )(lengths, block_mask, queries, keys, values, grad_out, gain.reshape(1, -1))


def solution(mesh):
    torus = Mesh(mesh.devices.reshape(NY, NX, NC, NZ), TOKEN_AXES)
    tokens = P(TOKEN_AXES, None)
    in_specs = (tokens,) * 4 + (P(), P(), P(TOKEN_AXES[:3], None))
    return jax.shard_map(
        local, mesh=torus, in_specs=in_specs, out_specs=(tokens,) * 4, check_vma=False
    )
```

time: 350 us -> 93.9 us (0.27)
  the two profiles are of different devices: /device:TPU:2 before, /device:TPU:1 now
where the time goes in v1:
time: 93.9 us; the launch traced here: 93.5 us
  Pallas kernels  84.2 us (90%)
  local copies, waits for them, and re-layouts  8.7 us (9%)
    pallas_call x1, Pallas kernels, local(): pl.pallas_call(kernel, out_shape=[jax.ShapeDtypeStruct(shape, BF16)] * 4,...  84.2 us
    unnamed x18, local copies, waits for them, and re-layouts  8.7 us

profile of v1, /device:TPU:1, one launch (start us, length us, event | category | flops | bytes accessed | tf_op | source)
XLA Modules:
  0.0 93.5 jit_solution(3560850063357070895)
XLA Ops:
  0.6 0.0 copy-start.5
  0.6 0.0 copy-start.6
  0.7 0.7 copy-done.5
  1.3 0.0 copy-done.6
  1.3 0.0 copy-start
  1.3 1.0 %copy-done = bf16[128,2048]{1,0:T(8,128)(2,1)S(1)} copy-done((bf16[128,2048]{1,0:T(8,128)(2,1)S(1)}, bf16[128,2048]{1,0:T(8,128)(2,1)}, u32[]{:S(2)}) %copy-start) | copy-done | bytes 524312
  2.4 0.0 copy-start.1
  2.4 1.0 %copy-done.1 = bf16[128,2048]{1,0:T(8,128)(2,1)S(1)} copy-done((bf16[128,2048]{1,0:T(8,128)(2,1)S(1)}, bf16[128,2048]{1,0:T(8,128)(2,1)}, u32[]{:S(2)}) %copy-start.1) | copy-done | bytes 524312
  3.4 0.0 copy-start.2
  3.4 1.0 %copy-done.2 = bf16[128,2048]{1,0:T(8,128)(2,1)S(1)} copy-done((bf16[128,2048]{1,0:T(8,128)(2,1)S(1)}, bf16[128,2048]{1,0:T(8,128)(2,1)}, u32[]{:S(2)}) %copy-start.2) | copy-done | bytes 524312
  4.4 0.0 copy-start.3
  4.4 1.0 %copy-done.3 = bf16[128,2048]{1,0:T(8,128)(2,1)S(1)} copy-done((bf16[128,2048]{1,0:T(8,128)(2,1)S(1)}, bf16[128,2048]{1,0:T(8,128)(2,1)}, u32[]{:S(2)}) %copy-start.3) | copy-done | bytes 524312
  5.5 0.0 copy-start.4
  5.5 0.7 copy-done.4
  6.2 84.2 %shard_map.102 = (bf16[128,2048]{1,0:T(8,128)(2,1)S(1)}, bf16[128,2048]{1,0:T(8,128)(2,1)S(1)}, bf16[128,2048]{1,0:T(8,128)(2,1)S(1)}, bf16[128,2048]{1,0:T(8,128)(2,1)S(1)}) custom-call(s32[4]{0:T(128)S(1)} %copy-done.6, s32[2,6]{1,0:T(2,128)S(1)} %copy-done.5, bf16[128,2048]{1,0:T(8,128)(2,1)S(1)} %copy-done, bf16[128,2048]{1,0:T(8,128)(2,1)S(1)} %copy-done.1, ...), custom_call_target="tpu_custom_call" | custom-call | tf_op jit(solution)/shard_map/pallas_call | solution.py:330
  90.4 0.8 copy.15
  91.1 0.8 copy.16
  91.9 0.8 copy.17
  92.7 0.8 copy.18
Async XLA Ops:
  0.6 0.7 copy-start.5
  0.6 0.7 copy-start.6
  1.3 1.0 %copy-start = (bf16[128,2048]{1,0:T(8,128)(2,1)S(1)}, bf16[128,2048]{1,0:T(8,128)(2,1)}, u32[]{:S(2)}) copy-start(bf16[128,2048]{1,0:T(8,128)(2,1)} %q_ref.1) | copy-start | bytes 1572868
  2.4 1.0 %copy-start.1 = (bf16[128,2048]{1,0:T(8,128)(2,1)S(1)}, bf16[128,2048]{1,0:T(8,128)(2,1)}, u32[]{:S(2)}) copy-start(bf16[128,2048]{1,0:T(8,128)(2,1)} %k_ref.1) | copy-start | bytes 1572868
  3.4 1.0 %copy-start.2 = (bf16[128,2048]{1,0:T(8,128)(2,1)S(1)}, bf16[128,2048]{1,0:T(8,128)(2,1)}, u32[]{:S(2)}) copy-start(bf16[128,2048]{1,0:T(8,128)(2,1)} %v_ref.1) | copy-start | bytes 1572868
  4.4 1.0 %copy-start.3 = (bf16[128,2048]{1,0:T(8,128)(2,1)S(1)}, bf16[128,2048]{1,0:T(8,128)(2,1)}, u32[]{:S(2)}) copy-start(bf16[128,2048]{1,0:T(8,128)(2,1)} %go_ref.1) | copy-start | bytes 1572868
  5.5 0.7 copy-start.4

commit v2 on v1

v2 whole, which is shorter than its diff:
```python
import jax
import jax.numpy as jnp
from jax import lax
from jax.experimental import pallas as pl
from jax.experimental.pallas import tpu as pltpu
from jax.sharding import Mesh
from jax.sharding import PartitionSpec as P

HEADS = 16
DH = 128
GROUP = 512
BLOCK = 128
EPS = 1e-06
F32 = jnp.float32
BF16 = jnp.bfloat16
TOKEN_AXES = ("cy", "cx", "cc", "head")
NY, NX, NC, NZ = 4, 4, 2, 8
CHIP = NC * NZ
MESH_ID = pl.DeviceIdType.MESH
CHUNKS = 4
FAR_FIRST = True
SKEW = True
ROWS = DH // CHUNKS


def mm(a, b, dims):
    return lax.dot_general(a, b, (dims, ((), ())), preferred_element_type=F32)


NN = ((1,), (0,))
NT = ((1,), (1,))
TN = ((0,), (0,))


def kernel(
    lengths_hbm, mask_hbm, q_hbm, k_hbm, v_hbm, go_hbm, gain_hbm,
    out_ref, gq_ref, gk_ref, gv_ref,
    lengths, block_mask, q_ref, k_ref, v_ref, go_ref, gain_ref, in_sems,
    mask_mine, mask_all, probs, gprobs, diag, acc_k, acc_v, d_ref,
    m_loc, m_own, x_own, x_loc, n_loc, n_own, y_own, y_loc,
    tot_x, rec_x, tot_y, rec_y, entering,
    a_send, a_recv, b_send, b_recv, x_send, x_recv, y_send, y_recv, mask_send, mask_recv,
):
    iy, ix, ic, iz = (lax.axis_index(a) for a in TOKEN_AXES)
    chip = iy * NX + ix
    mine = ic * NZ + iz
    owner = iz * NC + ic
    base = chip * (CHIP * BLOCK)
    start = base + mine * BLOCK

    loads = [
        pltpu.make_async_copy(src, dst, in_sems.at[n])
        for n, (src, dst) in enumerate(
            (
                (lengths_hbm, lengths),
                (mask_hbm, block_mask),
                (k_hbm, k_ref),
                (v_hbm, v_ref),
                (q_hbm, q_ref),
                (gain_hbm, gain_ref),
                (go_hbm, go_ref),
            )
        )
    ]
    for load in loads:
        load.start()

    barrier = pltpu.get_barrier_semaphore()

    def peer(step):
        turn = (CHIP - step if FAR_FIRST else step)
        pair = turn // NC
        away = (pair + 1) // 2
        z = lax.rem(iz + jnp.where(lax.rem(pair, 2) == 1, away, NZ - away), NZ)
        c = lax.rem(ic + turn, NC)
        return z * NC + c, {"head": z, "cc": c}

    def greet(step, carry):
        pl.semaphore_signal(barrier, 1, device_id=peer(step)[1], device_id_type=MESH_ID)
        return carry

    lax.fori_loop(1, CHIP, greet, 0)
    for step in range(1, NX):
        pl.semaphore_signal(
            barrier, 1, device_id={"cx": lax.rem(ix + step, NX)}, device_id_type=MESH_ID
        )
    for step in range(1, NY):
        pl.semaphore_signal(
            barrier, 1, device_id={"cy": lax.rem(iy + step, NY)}, device_id_type=MESH_ID
        )

    loads[0].wait()
    loads[1].wait()
    b1 = lengths[0]
    b2 = b1 + lengths[1]
    b3 = b2 + lengths[2]

    def seg(p):
        return (
            (p >= b1).astype(jnp.int32) + (p >= b2).astype(jnp.int32) + (p >= b3).astype(jnp.int32)
        )

    def same(a, b):
        return (a == b).astype(F32)

    for g in range(2):
        for n in range(6):
            mask_mine[8 * g + n : 8 * g + n + 1, :] = jnp.full(
                (1, DH), block_mask[g, n].astype(F32), F32
            )

    rows = lax.broadcasted_iota(jnp.int32, (BLOCK, BLOCK), 0)
    cols = lax.broadcasted_iota(jnp.int32, (BLOCK, BLOCK), 1)
    seg_r = seg(start + rows)
    seg_c = seg(start + cols)
    weight = jnp.where((seg_r == seg_c) & (cols <= rows), 1.0, 0.0).astype(F32)
    ends = jnp.where(seg_r == seg(start + BLOCK - 1), 1.0, 0.0).astype(BF16)
    starts = jnp.where(seg_r == seg(start), 1.0, 0.0).astype(BF16)
    before = jnp.where(seg_r == seg(start - 1), 1.0, 0.0).astype(BF16)
    after = jnp.where(seg_r == seg(start + BLOCK), 1.0, 0.0).astype(BF16)

    def col(h):
        return slice(h * DH, (h + 1) * DH)

    with jax.named_scope("load_kv"):
        loads[2].wait()
        loads[3].wait()
    with jax.named_scope("make_m"):
        for h in range(HEADS):
            m_loc[h] = mm(k_ref[:, col(h)] * ends, v_ref[:, col(h)], TN).astype(BF16)

    with jax.named_scope("barrier"):
        pl.semaphore_wait(barrier, CHIP - 1 + NX - 1 + NY - 1)

    mask_copy = pltpu.make_async_remote_copy(
        src_ref=mask_mine,
        dst_ref=mask_all.at[ic],
        send_sem=mask_send,
        recv_sem=mask_recv,
        device_id={"cc": 1 - ic},
        device_id_type=MESH_ID,
    )
    mask_copy.start()
    mask_all[ic] = mask_mine[...]

    def chunk(c):
        return pl.ds(c * ROWS, ROWS)

    def scatter_copy(src, dst, c, step, phase):
        e, to = peer(step)
        return pltpu.make_async_remote_copy(
            src_ref=src.at[e, chunk(c)],
            dst_ref=dst.at[mine, chunk(c)],
            send_sem=a_send.at[phase, c],
            recv_sem=a_recv.at[phase, c],
            device_id=to,
            device_id_type=MESH_ID,
        )

    def gather_copy(src, dst, c, step, phase):
        e, to = peer(step)
        r = lax.rem(e, NC) * NZ + e // NC
        return pltpu.make_async_remote_copy(
            src_ref=src.at[r, chunk(c)],
            dst_ref=dst.at[owner, chunk(c)],
            send_sem=b_send.at[phase, c],
            recv_sem=b_recv.at[phase, c],
            device_id=to,
            device_id_type=MESH_ID,
        )

    def start_scatter(src, dst, phase):
        for c in range(CHUNKS):

            def go(step, carry):
                scatter_copy(src, dst, c, step, phase).start()
                return carry

            lax.fori_loop(1, CHIP, go, 0)
        dst[mine] = src[owner]

    others = pl.ds(0, CHIP - 1)

    def wait_square(src, dst, c, phase, send, recv):
        pltpu.make_async_remote_copy(
            src_ref=src.at[others, chunk(c)],
            dst_ref=dst.at[others, chunk(c)],
            send_sem=send.at[phase, c],
            recv_sem=recv.at[phase, c],
            device_id=peer(1)[1],
            device_id_type=MESH_ID,
        ).wait()

    def start_gather(src, dst, c, phase):
        def go(step, carry):
            gather_copy(src, dst, c, step, phase).start()
            return carry

        lax.fori_loop(1, CHIP, go, 0)
        dst[owner, chunk(c)] = src[mine, chunk(c)]

    def send_line(total, slots, c, phase, axis, me, size, send, recv):
        for step in range(1, size):
            pltpu.make_async_remote_copy(
                src_ref=total.at[phase, chunk(c)],
                dst_ref=slots.at[phase, me, chunk(c)],
                send_sem=send.at[phase, c],
                recv_sem=recv.at[phase, c],
                device_id={axis: lax.rem(me + (size - step if FAR_FIRST else step), size)},
                device_id_type=MESH_ID,
            ).start()
        slots[phase, me, chunk(c)] = total[phase, chunk(c)]

    def wait_line(slots, c, phase, axis, me, size, send, recv):
        rest = slots.at[phase, pl.ds(0, size - 1), chunk(c)]
        pltpu.make_async_remote_copy(
            src_ref=rest,
            dst_ref=rest,
            send_sem=send.at[phase, c],
            recv_sem=recv.at[phase, c],
            device_id={axis: lax.rem(me + 1, size)},
            device_id_type=MESH_ID,
        ).wait()

    chip_len = CHIP * BLOCK
    row_len = NX * chip_len
    row_at = iy * row_len
    along_x = ("cx", ix, NX, x_send, x_recv)
    along_y = ("cy", iy, NY, y_send, y_recv)

    def marks(phase):
        forward = phase == 0
        lo = [base + r * BLOCK for r in range(CHIP)]
        edge = [seg(p + BLOCK - 1) if forward else seg(p) for p in lo]
        want = [seg(p - 1) if forward else seg(p + BLOCK) for p in lo]
        enter = seg(base - 1) if forward else seg(base + chip_len)
        return forward, edge, want, enter

    def edge_of(forward, at, size):
        return seg(at + size - 1) if forward else seg(at)

    def stage_x(own, c, phase):
        forward, edge, _, _ = marks(phase)
        last = CHIP - 1 if forward else 0
        total = own[last, chunk(c)].astype(F32)
        for r in range(CHIP):
            if r != last:
                total += same(edge[r], edge[last]) * own[r, chunk(c)].astype(F32)
        tot_x[phase, chunk(c)] = total
        send_line(tot_x, rec_x, c, phase, *along_x)

    def stage_y(c, phase):
        forward, _, _, enter = marks(phase)
        wait_line(rec_x, c, phase, *along_x)
        row_edge = edge_of(forward, row_at, row_len)
        row_total = jnp.zeros((ROWS, DH), F32)
        partial = jnp.zeros((ROWS, DH), F32)
        for x in range(NX):
            part = rec_x[phase, x, chunk(c)]
            its = edge_of(forward, row_at + x * chip_len, chip_len)
            row_total += same(its, row_edge) * part
            passed = (x < ix) if forward else (x > ix)
            partial += same(its, enter) * passed.astype(F32) * part
        tot_y[phase, chunk(c)] = row_total
        send_line(tot_y, rec_y, c, phase, *along_y)
        entering[phase, chunk(c)] = partial

    def stage_out(own, result, c, phase):
        forward, edge, want, enter = marks(phase)
        wait_line(rec_y, c, phase, *along_y)
        state = entering[phase, chunk(c)]
        for y in range(NY):
            its = edge_of(forward, y * row_len, row_len)
            passed = (y < iy) if forward else (y > iy)
            state += same(its, enter) * passed.astype(F32) * rec_y[phase, y, chunk(c)]

        def block(r):
            return own[r, chunk(c)].astype(F32)

        groups = range(CHIP // 4)
        reach = enter
        for g in groups if forward else reversed(groups):
            inner = range(4) if forward else (3, 2, 1, 0)
            seen = []
            for i in inner:
                r = 4 * g + i
                value = same(reach, want[r]) * state
                for j in seen:
                    hi, lo = (i, j) if forward else (j, i)
                    slot = 8 * (g % 2) + hi * (hi - 1) // 2 + lo
                    pair = mask_all[g // 2, slot : slot + 1, :] * same(edge[4 * g + j], want[r])
                    value += pair * block(4 * g + j)
                result[r, chunk(c)] = value.astype(BF16)
                seen.append(i)
            far = 4 * g + (3 if forward else 0)
            state = same(reach, edge[far]) * state
            for i in inner:
                state += same(edge[4 * g + i], edge[far]) * block(4 * g + i)
            reach = edge[far]

    def spread(loc, own, result, back, phase):
        def first(c):
            with jax.named_scope("wait_scatter"):
                wait_square(loc, own, c, phase, a_send, a_recv)
            with jax.named_scope("stage_x"):
                stage_x(own, c, phase)

        def second(c):
            with jax.named_scope("stage_y"):
                stage_y(c, phase)

        def third(c):
            with jax.named_scope("stage_out"):
                stage_out(own, result, c, phase)
            with jax.named_scope("start_gather"):
                start_gather(result, back, c, phase)

        if SKEW:
            for s in range(CHUNKS + 2):
                if s < CHUNKS:
                    first(s)
                if 0 <= s - 1 < CHUNKS:
                    second(s - 1)
                if 0 <= s - 2 < CHUNKS:
                    third(s - 2)
        else:
            for s in range(CHUNKS):
                first(s)
                second(s)
                third(s)
        for c in range(CHUNKS):
            with jax.named_scope("wait_gather"):
                wait_square(result, back, c, phase, b_send, b_recv)

    with jax.named_scope("start_scatter"):
        start_scatter(m_loc, m_own, 0)
    for load in loads[4:]:
        load.wait()
    with jax.named_scope("diag"):
        for h in range(HEADS):
            p = (mm(q_ref[:, col(h)], k_ref[:, col(h)], NT) * weight).astype(BF16)
            probs[h] = p
            diag[:, col(h)] = mm(p, v_ref[:, col(h)], NN)
    mask_copy.wait()
    spread(m_loc, m_own, x_own, x_loc, 0)

    with jax.named_scope("raw"):
        total_sq = jnp.zeros((BLOCK, DH), F32)
        total_gr = jnp.zeros((BLOCK, DH), F32)
        for h in range(HEADS):
            raw = (
                diag[:, col(h)] + mm(q_ref[:, col(h)] * before, x_loc[h], NN)
            ).astype(BF16).astype(F32)
            diag[:, col(h)] = raw
            scaled = go_ref[:, col(h)].astype(F32) * gain_ref[:, col(h)]
            total_sq += raw * raw
            total_gr += scaled * raw
    with jax.named_scope("norm"):
        width = HEADS * DH
        inv = 1.0 / jnp.sqrt(jnp.sum(total_sq, axis=1, keepdims=True) / width + EPS)
        cross = jnp.sum(total_gr, axis=1, keepdims=True) * inv / width
        for h in range(HEADS):
            normed = diag[:, col(h)] * inv
            scaled = go_ref[:, col(h)].astype(F32) * gain_ref[:, col(h)]
            out_ref[:, col(h)] = (normed * gain_ref[:, col(h)]).astype(BF16)
            d = ((scaled - normed * cross) * inv).astype(BF16)
            d_ref[:, col(h)] = d
            n_loc[h] = mm(q_ref[:, col(h)] * starts, d, TN).astype(BF16)
    with jax.named_scope("start_scatter"):
        start_scatter(n_loc, n_own, 1)

    with jax.named_scope("bdiag"):
        for h in range(HEADS):
            d = d_ref[:, col(h)]
            gp = (mm(d, v_ref[:, col(h)], NT) * weight).astype(BF16)
            gq_ref[:, col(h)] = (
                mm(gp, k_ref[:, col(h)], NN) + mm(d * before, x_loc[h], NT)
            ).astype(BF16)
            acc_k[:, col(h)] = mm(gp, q_ref[:, col(h)], TN)
            acc_v[:, col(h)] = mm(probs[h], d, TN)
    spread(n_loc, n_own, y_own, y_loc, 1)
    with jax.named_scope("final"):
        for h in range(HEADS):
            y = y_loc[h]
            gk_ref[:, col(h)] = (acc_k[:, col(h)] + mm(v_ref[:, col(h)] * after, y, NT)).astype(BF16)
            gv_ref[:, col(h)] = (acc_v[:, col(h)] + mm(k_ref[:, col(h)] * after, y, NN)).astype(BF16)


def store(*refs):
    sems = refs[8]
    copies = [pltpu.make_async_copy(refs[n], refs[4 + n], sems.at[n]) for n in range(4)]
    for copy in copies:
        copy.start()
    for copy in copies:
        copy.wait()


def local(queries, keys, values, grad_out, gain, lengths, block_mask):
    shape = queries.shape
    vmem = pl.BlockSpec(memory_space=pltpu.VMEM)
    hbm = pl.BlockSpec(memory_space=pltpu.HBM)
    square = (HEADS, DH, DH)
    dma = pltpu.SemaphoreType.DMA
    results = pl.pallas_call(
        kernel,
        out_shape=[jax.ShapeDtypeStruct(shape, BF16)] * 4,
        in_specs=[hbm] * 7,
        out_specs=[vmem] * 4,
        scratch_shapes=[pltpu.SMEM((4,), jnp.int32), pltpu.SMEM((2, 6), jnp.int32)]
        + [pltpu.VMEM(shape, BF16)] * 4
        + [
            pltpu.VMEM((1, shape[1]), F32),
            dma((7,)),
            pltpu.VMEM((16, DH), F32),
            pltpu.VMEM((2, 16, DH), F32),
            pltpu.VMEM(square, BF16),
            pltpu.VMEM((8, DH), BF16),
            pltpu.VMEM(shape, F32),
            pltpu.VMEM(shape, F32),
            pltpu.VMEM(shape, F32),
            pltpu.VMEM(shape, BF16),
        ]
        + [pltpu.VMEM(square, BF16)] * 8
        + [
            pltpu.VMEM((2, DH, DH), F32),
            pltpu.VMEM((2, NX, DH, DH), F32),
            pltpu.VMEM((2, DH, DH), F32),
            pltpu.VMEM((2, NY, DH, DH), F32),
            pltpu.VMEM((2, DH, DH), F32),
            dma((2, CHUNKS)),
            dma((2, CHUNKS)),
            dma((2, CHUNKS)),
            dma((2, CHUNKS)),
            dma((2, CHUNKS)),
            dma((2, CHUNKS)),
            dma((2, CHUNKS)),
            dma((2, CHUNKS)),
            dma,
            dma,
        ],
        compiler_params=pltpu.CompilerParams(
            collective_id=0, has_side_effects=True, vmem_limit_bytes=40 * 1024 * 1024
        ),
    )(
        *(
            pltpu.with_memory_space_constraint(a, pltpu.HBM)
            for a in (lengths, block_mask, queries, keys, values, grad_out, gain.reshape(1, -1))
        )
    )
    return pl.pallas_call(
        store,
        out_shape=[jax.ShapeDtypeStruct(shape, BF16)] * 4,
        in_specs=[vmem] * 4,
        out_specs=[hbm] * 4,
        scratch_shapes=[dma((4,))],
    )(*(pltpu.with_memory_space_constraint(r, pltpu.VMEM) for r in results))


def solution(mesh):
    torus = Mesh(mesh.devices.reshape(NY, NX, NC, NZ), TOKEN_AXES)
    tokens = P(TOKEN_AXES, None)
    in_specs = (tokens,) * 4 + (P(), P(), P(TOKEN_AXES[:3], None))
    return jax.shard_map(
        local, mesh=torus, in_specs=in_specs, out_specs=(tokens,) * 4, check_vma=False
    )
```

time: 93.9 us -> 68.8 us (0.73)
  Pallas kernels: 84.2 us -> 68.1 us
  local copies, waits for them, and re-layouts: 8.7 us -> 0 us
    pallas_call x1, Pallas kernels: 84.2 us -> 66.7 us  [local(): pl.pallas_call(kernel, out_shape=[jax.ShapeDtypeStruct(shape, BF16)] * 4,...]
    unnamed x18 -> x0, local copies, waits for them, and re-layouts: 8.7 us -> none
    pallas_call x0 -> x1, Pallas kernels: none -> 1.35 us  [local(): pl.pallas_call(store, out_shape=[jax.ShapeDtypeStruct(shape, BF16)] * 4,...]
where the time goes in v2:
time: 68.8 us; the launch traced here: 68.7 us
  Pallas kernels  68.1 us (99%)
    pallas_call x1, Pallas kernels, local(): pl.pallas_call(kernel, out_shape=[jax.ShapeDtypeStruct(shape, BF16)] * 4,...  66.7 us

profile of v2, /device:TPU:1, one launch (start us, length us, event | category | flops | bytes accessed | tf_op | source)
XLA Modules:
  0.0 68.7 jit_solution(8570381134052647186)
XLA Ops:
  0.6 66.7 %shard_map.102 = (bf16[128,2048]{1,0:T(8,128)(2,1)S(1)}, bf16[128,2048]{1,0:T(8,128)(2,1)S(1)}, bf16[128,2048]{1,0:T(8,128)(2,1)S(1)}, bf16[128,2048]{1,0:T(8,128)(2,1)S(1)}) custom-call(s32[4]{0:T(128)} %lengths_hbm.1, s32[2,6]{1,0:T(2,128)} %mask_hbm.1, bf16[128,2048]{1,0:T(8,128)(2,1)} %q_hbm.1, bf16[128,2048]{1,0:T(8,128)(2,1)} %k_hbm.1, ...), custom_call_target="tpu_custom_call" | custom-call | tf_op jit(solution)/shard_map/pallas_call | solution.py:404
  67.4 1.3 %shard_map.103 = (bf16[128,2048]{1,0:T(8,128)(2,1)}, bf16[128,2048]{1,0:T(8,128)(2,1)}, bf16[128,2048]{1,0:T(8,128)(2,1)}, bf16[128,2048]{1,0:T(8,128)(2,1)}) custom-call(bf16[128,2048]{1,0:T(8,128)(2,1)S(1)} %get-tuple-element.8.refs_0_, bf16[128,2048]{1,0:T(8,128)(2,1)S(1)} %get-tuple-element.9.refs_1_, bf16[128,2048]{1,0:T(8,128)(2,1)S(1)} %get-tuple-element.10.refs_2_, ...), custom_call_target="tpu_custom_call" | custom-call | tf_op jit(solution)/shard_map/pallas_call | solution.py:450

commit v3 on v2

--- a/solution.py
+++ b/solution.py
@@ -17,10 +17,11 @@
 NY, NX, NC, NZ = 4, 4, 2, 8
 CHIP = NC * NZ
 MESH_ID = pl.DeviceIdType.MESH
-CHUNKS = 4
-FAR_FIRST = True
-SKEW = True
-ROWS = DH // CHUNKS
+SIZES = (16,) * 8
+LAG = 2
+ORDER = (4, 3, 5, 2, 6, 1, 7, 0)
+CHUNKS = len(SIZES)
+FIRST = [sum(SIZES[:c]) for c in range(CHUNKS)]
 
 
 def mm(a, b, dims):
@@ -34,9 +35,9 @@
 
 def kernel(
     lengths_hbm, mask_hbm, q_hbm, k_hbm, v_hbm, go_hbm, gain_hbm,
-    out_ref, gq_ref, gk_ref, gv_ref,
-    lengths, block_mask, q_ref, k_ref, v_ref, go_ref, gain_ref, in_sems,
-    mask_mine, mask_all, probs, gprobs, diag, acc_k, acc_v, d_ref,
+    out_ref, gq_ref, k_ref, v_ref, acc_k, acc_v, y_out, after_out,
+    lengths, block_mask, q_ref, go_ref, gain_ref, in_sems,
+    mask_mine, mask_all, probs, diag, d_ref,
     m_loc, m_own, x_own, x_loc, n_loc, n_own, y_own, y_loc,
     tot_x, rec_x, tot_y, rec_y, entering,
     a_send, a_recv, b_send, b_recv, x_send, x_recv, y_send, y_recv, mask_send, mask_recv,
@@ -52,10 +53,10 @@
         pltpu.make_async_copy(src, dst, in_sems.at[n])
         for n, (src, dst) in enumerate(
             (
+                (k_hbm, k_ref),
+                (v_hbm, v_ref),
                 (lengths_hbm, lengths),
                 (mask_hbm, block_mask),
-                (k_hbm, k_ref),
-                (v_hbm, v_ref),
                 (q_hbm, q_ref),
                 (gain_hbm, gain_ref),
                 (go_hbm, go_ref),
@@ -68,11 +69,8 @@
     barrier = pltpu.get_barrier_semaphore()
 
     def peer(step):
-        turn = (CHIP - step if FAR_FIRST else step)
-        pair = turn // NC
-        away = (pair + 1) // 2
-        z = lax.rem(iz + jnp.where(lax.rem(pair, 2) == 1, away, NZ - away), NZ)
-        c = lax.rem(ic + turn, NC)
+        z = lax.rem(iz + step // NC, NZ)
+        c = lax.rem(ic + step, NC)
         return z * NC + c, {"head": z, "cc": c}
 
     def greet(step, carry):
@@ -89,8 +87,8 @@
             barrier, 1, device_id={"cy": lax.rem(iy + step, NY)}, device_id_type=MESH_ID
         )
 
-    loads[0].wait()
-    loads[1].wait()
+    loads[2].wait()
+    loads[3].wait()
     b1 = lengths[0]
     b2 = b1 + lengths[1]
     b3 = b2 + lengths[2]
@@ -117,14 +115,13 @@
     ends = jnp.where(seg_r == seg(start + BLOCK - 1), 1.0, 0.0).astype(BF16)
     starts = jnp.where(seg_r == seg(start), 1.0, 0.0).astype(BF16)
     before = jnp.where(seg_r == seg(start - 1), 1.0, 0.0).astype(BF16)
-    after = jnp.where(seg_r == seg(start + BLOCK), 1.0, 0.0).astype(BF16)
 
     def col(h):
         return slice(h * DH, (h + 1) * DH)
 
     with jax.named_scope("load_kv"):
-        loads[2].wait()
-        loads[3].wait()
+        loads[0].wait()
+        loads[1].wait()
     with jax.named_scope("make_m"):
         for h in range(HEADS):
             m_loc[h] = mm(k_ref[:, col(h)] * ends, v_ref[:, col(h)], TN).astype(BF16)
@@ -144,14 +141,14 @@
     mask_all[ic] = mask_mine[...]
 
     def chunk(c):
-        return pl.ds(c * ROWS, ROWS)
+        return pl.ds(FIRST[c], SIZES[c])
 
     def scatter_copy(src, dst, c, step, phase):
         e, to = peer(step)
         return pltpu.make_async_remote_copy(
             src_ref=src.at[e, chunk(c)],
             dst_ref=dst.at[mine, chunk(c)],
-            send_sem=a_send.at[phase, c],
+            send_sem=a_send.at[phase],
             recv_sem=a_recv.at[phase, c],
             device_id=to,
             device_id_type=MESH_ID,
@@ -163,20 +160,21 @@
         return pltpu.make_async_remote_copy(
             src_ref=src.at[r, chunk(c)],
             dst_ref=dst.at[owner, chunk(c)],
-            send_sem=b_send.at[phase, c],
+            send_sem=b_send.at[phase],
             recv_sem=b_recv.at[phase, c],
             device_id=to,
             device_id_type=MESH_ID,
         )
 
+    def start_square(copy, src, dst, c, phase):
+        for away in ORDER:
+            for other in range(NC):
+                if away or other:
+                    copy(src, dst, c, away * NC + other, phase).start()
+
     def start_scatter(src, dst, phase):
         for c in range(CHUNKS):
-
-            def go(step, carry):
-                scatter_copy(src, dst, c, step, phase).start()
-                return carry
-
-            lax.fori_loop(1, CHIP, go, 0)
+            start_square(scatter_copy, src, dst, c, phase)
         dst[mine] = src[owner]
 
     others = pl.ds(0, CHIP - 1)
@@ -185,28 +183,46 @@
         pltpu.make_async_remote_copy(
             src_ref=src.at[others, chunk(c)],
             dst_ref=dst.at[others, chunk(c)],
-            send_sem=send.at[phase, c],
+            send_sem=send.at[phase],
             recv_sem=recv.at[phase, c],
             device_id=peer(1)[1],
             device_id_type=MESH_ID,
-        ).wait()
+        ).wait_recv()
+
+    def drain_square(src, dst, phase, send, recv):
+        pltpu.make_async_remote_copy(
+            src_ref=src.at[others],
+            dst_ref=dst.at[others],
+            send_sem=send.at[phase],
+            recv_sem=recv.at[phase, 0],
+            device_id=peer(1)[1],
+            device_id_type=MESH_ID,
+        ).wait_send()
+
+    def drain_line(slots, phase, axis, me, size, send, recv):
+        rest = slots.at[phase, pl.ds(0, size - 1)]
+        pltpu.make_async_remote_copy(
+            src_ref=rest,
+            dst_ref=rest,
+            send_sem=send.at[phase],
+            recv_sem=recv.at[phase, 0],
+            device_id={axis: lax.rem(me + 1, size)},
+            device_id_type=MESH_ID,
+        ).wait_send()
 
     def start_gather(src, dst, c, phase):
-        def go(step, carry):
-            gather_copy(src, dst, c, step, phase).start()
-            return carry
-
-        lax.fori_loop(1, CHIP, go, 0)
-        dst[owner, chunk(c)] = src[mine, chunk(c)]
+        start_square(gather_copy, src, dst, c, phase)
+        if c == CHUNKS - 1:
+            dst[owner] = src[mine]
 
     def send_line(total, slots, c, phase, axis, me, size, send, recv):
         for step in range(1, size):
             pltpu.make_async_remote_copy(
                 src_ref=total.at[phase, chunk(c)],
                 dst_ref=slots.at[phase, me, chunk(c)],
-                send_sem=send.at[phase, c],
+                send_sem=send.at[phase],
                 recv_sem=recv.at[phase, c],
-                device_id={axis: lax.rem(me + (size - step if FAR_FIRST else step), size)},
+                device_id={axis: lax.rem(me + size - step, size)},
                 device_id_type=MESH_ID,
             ).start()
         slots[phase, me, chunk(c)] = total[phase, chunk(c)]
@@ -216,11 +232,11 @@
         pltpu.make_async_remote_copy(
             src_ref=rest,
             dst_ref=rest,
-            send_sem=send.at[phase, c],
+            send_sem=send.at[phase],
             recv_sem=recv.at[phase, c],
             device_id={axis: lax.rem(me + 1, size)},
             device_id_type=MESH_ID,
-        ).wait()
+        ).wait_recv()
 
     chip_len = CHIP * BLOCK
     row_len = NX * chip_len
@@ -253,8 +269,8 @@
         forward, _, _, enter = marks(phase)
         wait_line(rec_x, c, phase, *along_x)
         row_edge = edge_of(forward, row_at, row_len)
-        row_total = jnp.zeros((ROWS, DH), F32)
-        partial = jnp.zeros((ROWS, DH), F32)
+        row_total = jnp.zeros((SIZES[c], DH), F32)
+        partial = jnp.zeros((SIZES[c], DH), F32)
         for x in range(NX):
             part = rec_x[phase, x, chunk(c)]
             its = edge_of(forward, row_at + x * chip_len, chip_len)
@@ -298,7 +314,7 @@
                 state += same(edge[4 * g + i], edge[far]) * block(4 * g + i)
             reach = edge[far]
 
-    def spread(loc, own, result, back, phase):
+    def spread(loc, own, result, back, phase, filler):
         def first(c):
             with jax.named_scope("wait_scatter"):
                 wait_square(loc, own, c, phase, a_send, a_recv)
@@ -315,19 +331,17 @@
             with jax.named_scope("start_gather"):
                 start_gather(result, back, c, phase)
 
-        if SKEW:
-            for s in range(CHUNKS + 2):
-                if s < CHUNKS:
-                    first(s)
-                if 0 <= s - 1 < CHUNKS:
-                    second(s - 1)
-                if 0 <= s - 2 < CHUNKS:
-                    third(s - 2)
-        else:
-            for s in range(CHUNKS):
+        for s in range(CHUNKS + 2 * LAG):
+            if s < CHUNKS:
                 first(s)
-                second(s)
-                third(s)
+            if 0 <= s - LAG < CHUNKS:
+                second(s - LAG)
+            if 0 <= s - 2 * LAG < CHUNKS:
+                third(s - 2 * LAG)
+            if s < 4:
+                with jax.named_scope("filler"):
+                    for h in range(4 * s, 4 * s + 4):
+                        filler(h)
         for c in range(CHUNKS):
             with jax.named_scope("wait_gather"):
                 wait_square(result, back, c, phase, b_send, b_recv)
@@ -336,13 +350,13 @@
         start_scatter(m_loc, m_own, 0)
     for load in loads[4:]:
         load.wait()
-    with jax.named_scope("diag"):
-        for h in range(HEADS):
-            p = (mm(q_ref[:, col(h)], k_ref[:, col(h)], NT) * weight).astype(BF16)
-            probs[h] = p
-            diag[:, col(h)] = mm(p, v_ref[:, col(h)], NN)
+    def forward_head(h):
+        p = (mm(q_ref[:, col(h)], k_ref[:, col(h)], NT) * weight).astype(BF16)
+        probs[h] = p
+        diag[:, col(h)] = mm(p, v_ref[:, col(h)], NN)
+
     mask_copy.wait()
-    spread(m_loc, m_own, x_own, x_loc, 0)
+    spread(m_loc, m_own, x_own, x_loc, 0, forward_head)
 
     with jax.named_scope("raw"):
         total_sq = jnp.zeros((BLOCK, DH), F32)
@@ -362,36 +376,59 @@
         for h in range(HEADS):
             normed = diag[:, col(h)] * inv
             scaled = go_ref[:, col(h)].astype(F32) * gain_ref[:, col(h)]
-            out_ref[:, col(h)] = (normed * gain_ref[:, col(h)]).astype(BF16)
             d = ((scaled - normed * cross) * inv).astype(BF16)
             d_ref[:, col(h)] = d
             n_loc[h] = mm(q_ref[:, col(h)] * starts, d, TN).astype(BF16)
     with jax.named_scope("start_scatter"):
         start_scatter(n_loc, n_own, 1)
 
-    with jax.named_scope("bdiag"):
-        for h in range(HEADS):
-            d = d_ref[:, col(h)]
-            gp = (mm(d, v_ref[:, col(h)], NT) * weight).astype(BF16)
-            gq_ref[:, col(h)] = (
-                mm(gp, k_ref[:, col(h)], NN) + mm(d * before, x_loc[h], NT)
-            ).astype(BF16)
-            acc_k[:, col(h)] = mm(gp, q_ref[:, col(h)], TN)
-            acc_v[:, col(h)] = mm(probs[h], d, TN)
-    spread(n_loc, n_own, y_own, y_loc, 1)
-    with jax.named_scope("final"):
-        for h in range(HEADS):
-            y = y_loc[h]
-            gk_ref[:, col(h)] = (acc_k[:, col(h)] + mm(v_ref[:, col(h)] * after, y, NT)).astype(BF16)
-            gv_ref[:, col(h)] = (acc_v[:, col(h)] + mm(k_ref[:, col(h)] * after, y, NN)).astype(BF16)
-
-
-def store(*refs):
-    sems = refs[8]
-    copies = [pltpu.make_async_copy(refs[n], refs[4 + n], sems.at[n]) for n in range(4)]
-    for copy in copies:
+    def backward_head(h):
+        d = d_ref[:, col(h)]
+        out_ref[:, col(h)] = (diag[:, col(h)] * inv * gain_ref[:, col(h)]).astype(BF16)
+        gp = (mm(d, v_ref[:, col(h)], NT) * weight).astype(BF16)
+        gq_ref[:, col(h)] = (
+            mm(gp, k_ref[:, col(h)], NN) + mm(d * before, x_loc[h], NT)
+        ).astype(BF16)
+        acc_k[:, col(h)] = mm(gp, q_ref[:, col(h)], TN)
+        acc_v[:, col(h)] = mm(probs[h], d, TN)
+
+    spread(n_loc, n_own, y_own, y_loc, 1, backward_head)
+    drain_square(m_loc, m_own, 0, a_send, a_recv)
+    drain_square(x_own, x_loc, 0, b_send, b_recv)
+    drain_square(n_loc, n_own, 1, a_send, a_recv)
+    drain_square(y_own, y_loc, 1, b_send, b_recv)
+    for phase in range(2):
+        drain_line(rec_x, phase, *along_x)
+        drain_line(rec_y, phase, *along_y)
+    after_out[...] = jnp.where(seg_r == seg(start + BLOCK), 1.0, 0.0).astype(BF16)
+    y_out[...] = y_loc[...]
+
+
+def finish(
+    out_ref, gq_ref, k_ref, v_ref, acc_k, acc_v, y_ref, after_ref,
+    out_hbm, gq_hbm, gk_hbm, gv_hbm,
+    gk_ref, gv_ref, sems,
+):
+    early = [
+        pltpu.make_async_copy(out_ref, out_hbm, sems.at[0]),
+        pltpu.make_async_copy(gq_ref, gq_hbm, sems.at[1]),
+    ]
+    for copy in early:
         copy.start()
-    for copy in copies:
+    after = after_ref[...]
+    for h in range(HEADS):
+        at = slice(h * DH, (h + 1) * DH)
+        gv_ref[:, at] = (acc_v[:, at] + mm(k_ref[:, at] * after, y_ref[h], NN)).astype(BF16)
+    late = [
+        pltpu.make_async_copy(gv_ref, gv_hbm, sems.at[2]),
+        pltpu.make_async_copy(gk_ref, gk_hbm, sems.at[3]),
+    ]
+    late[0].start()
+    for h in range(HEADS):
+        at = slice(h * DH, (h + 1) * DH)
+        gk_ref[:, at] = (acc_k[:, at] + mm(v_ref[:, at] * after, y_ref[h], NT)).astype(BF16)
+    late[1].start()
+    for copy in early + late:
         copy.wait()
 
 
@@ -401,22 +438,25 @@
     hbm = pl.BlockSpec(memory_space=pltpu.HBM)
     square = (HEADS, DH, DH)
     dma = pltpu.SemaphoreType.DMA
+    tokens = jax.ShapeDtypeStruct(shape, BF16)
+    sums = jax.ShapeDtypeStruct(shape, F32)
     results = pl.pallas_call(
         kernel,
-        out_shape=[jax.ShapeDtypeStruct(shape, BF16)] * 4,
+        out_shape=[tokens] * 4
+        + [sums] * 2
+        + [jax.ShapeDtypeStruct(square, BF16), jax.ShapeDtypeStruct((BLOCK, DH), BF16)],
         in_specs=[hbm] * 7,
-        out_specs=[vmem] * 4,
-        scratch_shapes=[pltpu.SMEM((4,), jnp.int32), pltpu.SMEM((2, 6), jnp.int32)]
-        + [pltpu.VMEM(shape, BF16)] * 4
-        + [
+        out_specs=[vmem] * 8,
+        scratch_shapes=[
+            pltpu.SMEM((4,), jnp.int32),
+            pltpu.SMEM((2, 6), jnp.int32),
+            pltpu.VMEM(shape, BF16),
+            pltpu.VMEM(shape, BF16),
             pltpu.VMEM((1, shape[1]), F32),
             dma((7,)),
             pltpu.VMEM((16, DH), F32),
             pltpu.VMEM((2, 16, DH), F32),
             pltpu.VMEM(square, BF16),
-            pltpu.VMEM((8, DH), BF16),
-            pltpu.VMEM(shape, F32),
-            pltpu.VMEM(shape, F32),
             pltpu.VMEM(shape, F32),
             pltpu.VMEM(shape, BF16),
         ]
@@ -427,19 +467,11 @@
             pltpu.VMEM((2, DH, DH), F32),
             pltpu.VMEM((2, NY, DH, DH), F32),
             pltpu.VMEM((2, DH, DH), F32),
-            dma((2, CHUNKS)),
-            dma((2, CHUNKS)),
-            dma((2, CHUNKS)),
-            dma((2, CHUNKS)),
-            dma((2, CHUNKS)),
-            dma((2, CHUNKS)),
-            dma((2, CHUNKS)),
-            dma((2, CHUNKS)),
-            dma,
-            dma,
-        ],
+        ]
+        + [dma((2,)), dma((2, CHUNKS))] * 4
+        + [dma, dma],
         compiler_params=pltpu.CompilerParams(
-            collective_id=0, has_side_effects=True, vmem_limit_bytes=40 * 1024 * 1024
+            collective_id=0, has_side_effects=True, vmem_limit_bytes=24 * 1024 * 1024
         ),
     )(
         *(
@@ -448,11 +480,12 @@
         )
     )
     return pl.pallas_call(
-        store,
-        out_shape=[jax.ShapeDtypeStruct(shape, BF16)] * 4,
-        in_specs=[vmem] * 4,
+        finish,
+        out_shape=[tokens] * 4,
+        in_specs=[vmem] * 8,
         out_specs=[hbm] * 4,
-        scratch_shapes=[dma((4,))],
+        scratch_shapes=[pltpu.VMEM(shape, BF16), pltpu.VMEM(shape, BF16), dma((4,))],
+        compiler_params=pltpu.CompilerParams(vmem_limit_bytes=16 * 1024 * 1024),
     )(*(pltpu.with_memory_space_constraint(r, pltpu.VMEM) for r in results))
 
 

time: 68.8 us -> 67.8 us (0.985)
  Pallas kernels: 68.1 us -> 67.1 us
    pallas_call x2, Pallas kernels: 68.1 us -> 67.1 us  [the longest x1 65.6 us: local(): pl.pallas_call(kernel, out_shape=[tokens] * 4 + [sums] * 2 + [jax.ShapeDt...]
where the time goes in v3:
time: 67.8 us; the launch traced here: 67.7 us
  Pallas kernels  67.1 us (99%)
    pallas_call x1, Pallas kernels, local(): pl.pallas_call(kernel, out_shape=[tokens] * 4 + [sums] * 2 + [jax.ShapeDt...  65.6 us
    pallas_call x1, Pallas kernels, local(): pl.pallas_call(finish, out_shape=[tokens] * 4, in_specs=[vmem] * 8, out_s...  1.49 us

profile of v3, /device:TPU:1, one launch (start us, length us, event | category | flops | bytes accessed | tf_op | source)
XLA Modules:
  0.0 67.7 jit_solution(6256810929693065992)
XLA Ops:
  0.6 65.6 %shard_map.102 = (bf16[128,2048]{1,0:T(8,128)(2,1)S(1)}, bf16[128,2048]{1,0:T(8,128)(2,1)S(1)}, bf16[128,2048]{1,0:T(8,128)(2,1)S(1)}, bf16[128,2048]{1,0:T(8,12...) custom-call(s32[4]{0:T(128)} %lengths_hbm.1, ...), custom_call_target="tpu_custom_call" | custom-call | tf_op jit(solution)/shard_map/pallas_call | solution.py:443
  66.2 1.5 %shard_map.103 = (bf16[128,2048]{1,0:T(8,128)(2,1)}, bf16[128,2048]{1,0:T(8,128)(2,1)}, bf16[128,2048]{1,0:T(8,128)(2,1)}, bf16[128,2048]{1,0:T(8,128)(2,1)}) custom-call(bf16[128,2048]{1,0:T(8,128)(2,1)S(1)} %get-tuple-element.12.out_ref, bf16[128,2048]{1,0:T(8,128)(2,1)S(1)} %get-tuple-element.13.gq_ref, bf16[128,2048]{1,0:T(8,128)(2,1)S(1)} %get-tuple-element.14.k_ref, ...), custom_call_target="tpu_custom_call" | custom-call | tf_op jit(solution)/shard_map/pallas_call | solution.py:482

commit v4 on v3

--- a/solution.py
+++ b/solution.py
@@ -19,6 +19,7 @@
 MESH_ID = pl.DeviceIdType.MESH
 SIZES = (16,) * 8
 LAG = 2
+EARLY = False
 ORDER = (4, 3, 5, 2, 6, 1, 7, 0)
 CHUNKS = len(SIZES)
 FIRST = [sum(SIZES[:c]) for c in range(CHUNKS)]
@@ -73,11 +74,12 @@
         c = lax.rem(ic + step, NC)
         return z * NC + c, {"head": z, "cc": c}
 
-    def greet(step, carry):
-        pl.semaphore_signal(barrier, 1, device_id=peer(step)[1], device_id_type=MESH_ID)
-        return carry
-
-    lax.fori_loop(1, CHIP, greet, 0)
+    for away in ORDER:
+        for other in range(NC):
+            if away or other:
+                pl.semaphore_signal(
+                    barrier, 1, device_id=peer(away * NC + other)[1], device_id_type=MESH_ID
+                )
     for step in range(1, NX):
         pl.semaphore_signal(
             barrier, 1, device_id={"cx": lax.rem(ix + step, NX)}, device_id_type=MESH_ID
@@ -88,7 +90,6 @@
         )
 
     loads[2].wait()
-    loads[3].wait()
     b1 = lengths[0]
     b2 = b1 + lengths[1]
     b3 = b2 + lengths[2]
@@ -100,12 +101,6 @@
 
     def same(a, b):
         return (a == b).astype(F32)
-
-    for g in range(2):
-        for n in range(6):
-            mask_mine[8 * g + n : 8 * g + n + 1, :] = jnp.full(
-                (1, DH), block_mask[g, n].astype(F32), F32
-            )
 
     rows = lax.broadcasted_iota(jnp.int32, (BLOCK, BLOCK), 0)
     cols = lax.broadcasted_iota(jnp.int32, (BLOCK, BLOCK), 1)
@@ -128,17 +123,6 @@
 
     with jax.named_scope("barrier"):
         pl.semaphore_wait(barrier, CHIP - 1 + NX - 1 + NY - 1)
-
-    mask_copy = pltpu.make_async_remote_copy(
-        src_ref=mask_mine,
-        dst_ref=mask_all.at[ic],
-        send_sem=mask_send,
-        recv_sem=mask_recv,
-        device_id={"cc": 1 - ic},
-        device_id_type=MESH_ID,
-    )
-    mask_copy.start()
-    mask_all[ic] = mask_mine[...]
 
     def chunk(c):
         return pl.ds(FIRST[c], SIZES[c])
@@ -332,9 +316,11 @@
                 start_gather(result, back, c, phase)
 
         for s in range(CHUNKS + 2 * LAG):
+            if EARLY and 0 <= s - LAG < CHUNKS:
+                second(s - LAG)
             if s < CHUNKS:
                 first(s)
-            if 0 <= s - LAG < CHUNKS:
+            if not EARLY and 0 <= s - LAG < CHUNKS:
                 second(s - LAG)
             if 0 <= s - 2 * LAG < CHUNKS:
                 third(s - 2 * LAG)
@@ -348,13 +334,28 @@
 
     with jax.named_scope("start_scatter"):
         start_scatter(m_loc, m_own, 0)
-    for load in loads[4:]:
+    for load in loads[3:]:
         load.wait()
+    for g in range(2):
+        for n in range(6):
+            mask_mine[8 * g + n : 8 * g + n + 1, :] = jnp.full(
+                (1, DH), block_mask[g, n].astype(F32), F32
+            )
     def forward_head(h):
         p = (mm(q_ref[:, col(h)], k_ref[:, col(h)], NT) * weight).astype(BF16)
         probs[h] = p
         diag[:, col(h)] = mm(p, v_ref[:, col(h)], NN)
 
+    mask_copy = pltpu.make_async_remote_copy(
+        src_ref=mask_mine,
+        dst_ref=mask_all.at[ic],
+        send_sem=mask_send,
+        recv_sem=mask_recv,
+        device_id={"cc": 1 - ic},
+        device_id_type=MESH_ID,
+    )
+    mask_copy.start()
+    mask_all[ic] = mask_mine[...]
     mask_copy.wait()
     spread(m_loc, m_own, x_own, x_loc, 0, forward_head)
 

time: 67.8 us -> 67.7 us (level)
  no operation moved by 1% of the time
where the time goes in v4:
time: 67.7 us; the launch traced here: 67.6 us
  Pallas kernels  66.9 us (99%)
    pallas_call x1, Pallas kernels, local(): pl.pallas_call(kernel, out_shape=[tokens] * 4 + [sums] * 2 + [jax.ShapeDt...  65.5 us
    pallas_call x1, Pallas kernels, local(): pl.pallas_call(finish, out_shape=[tokens] * 4, in_specs=[vmem] * 8, out_s...  1.49 us

profile of v4, /device:TPU:1, one launch (start us, length us, event | category | flops | bytes accessed | tf_op | source)
XLA Modules:
  0.0 67.6 jit_solution(1677157882725841340)
XLA Ops:
  0.6 65.5 %shard_map.102 = (bf16[128,2048]{1,0:T(8,128)(2,1)S(1)}, bf16[128,2048]{1,0:T(8,128)(2,1)S(1)}, bf16[128,2048]{1,0:T(8,128)(2,1)S(1)}, bf16[128,2048]{1,0:T(8,12...) custom-call(s32[4]{0:T(128)} %lengths_hbm.1, ...), custom_call_target="tpu_custom_call" | custom-call | tf_op jit(solution)/shard_map/pallas_call | solution.py:444
  66.1 1.5 %shard_map.103 = (bf16[128,2048]{1,0:T(8,128)(2,1)}, bf16[128,2048]{1,0:T(8,128)(2,1)}, bf16[128,2048]{1,0:T(8,128)(2,1)}, bf16[128,2048]{1,0:T(8,128)(2,1)}) custom-call(bf16[128,2048]{1,0:T(8,128)(2,1)S(1)} %get-tuple-element.12.out_ref, bf16[128,2048]{1,0:T(8,128)(2,1)S(1)} %get-tuple-element.13.gq_ref, bf16[128,2048]{1,0:T(8,128)(2,1)S(1)} %get-tuple-element.14.k_ref, ...), custom_call_target="tpu_custom_call" | custom-call | tf_op jit(solution)/shard_map/pallas_call | solution.py:483
